TPU v7x, 32 devices: a whole 2x2x4 slice. The times are simulated.
32 devices in a mesh: lat: 8 (over z, y), rad: 4 (over x, core).
Axes of the slice: x: 2, y: 2, z: 4, core: 2. Of those that a mesh axis runs over, the one named last changes fastest.
Arguments:
- source: float32 [128, 32768], P('rad', 'lat'), may hold values from -6 to 6
- to_modes: float32 [128, 128], replicated, may hold values from -0.5 to 0.5
- from_modes: float32 [128, 128], replicated, may hold values from -0.5 to 0.5
- eigenvalue: float32 [128], replicated, may hold values from 0.1 to 20
- shifts: float32 [32768], P('lat'), may hold values from 0.5 to 2
- weights: float32 [31, 32768], P(None, 'lat'), may hold values from 0.02 to 0.12
- neighbors: int32 [31, 256], P(None, 'lat'), may hold values from -8 to 8, as said below
Outputs:
- smoothed: float32 [128, 32768], P('rad', 'lat')
- residual_norm: float32 [128], P('rad')
Inputs may be any that keep to these rules, and one draw needn't show every extreme that they name: `neighbors`: every entry is nonzero; some entry equals -8.
All inputs are finite; a program needn't handle non-finite values.
Results may differ from a plain program's by a relative error of at most 0.000073.
Values sent between devices are 32-bit elements; how exact they have to be, the bound alone decides.
A program may use at most 64 MiB of HBM per device.

v0:
```python
import functools

import jax
import jax.numpy as jnp
from jax import lax
from jax.experimental import pallas as pl
from jax.experimental.pallas import tpu as pltpu
from jax.sharding import PartitionSpec as P

BLOCK = 128
HALO = 8
CHUNKS = 4
GROUP = 8
CORES = 2
HIGHEST = lax.Precision.HIGHEST
MESH = pl.DeviceIdType.MESH


def dot(a, b):
    return jnp.dot(a, b, precision=HIGHEST, preferred_element_type=jnp.float32)


def kernel(
    L, R, S,
    src, w_hbm, to_hbm, from_hbm, eig_hbm, shift_hbm, nbr_hbm,
    out, res_ref,
    gathered, wv, wr, outer1, inner1, outer2, inner2, others, modal, image, twice, eig_t, coef, part,
    rows, s1, s2, s3, to_ref, from_ref, eig_ref, nbr_ref,
    in_sem, own_sem, w_sem, ag_send, ag_recv,
    o1_send, o1_recv, i1_send, i1_recv, o2_send, o2_recv, i2_send, i2_recv, x_send, x_recv,
    im_send, im_recv, s1_send, s1_recv, s2_send, s2_recv, s3_send, s3_recv,
    out_send, out_recv, out_sem,
):
    T = CHUNKS
    X = R // CORES
    M = L * CORES
    slab, nodes = src.shape
    K = slab * CORES
    half = nodes // CORES
    NB = half // BLOCK
    CB = NB // T
    HC = HALO // CB
    CW = CB * BLOCK
    E = NB + HALO
    A = -(-S // GROUP)
    lat = lax.axis_index("lat")
    rad = lax.axis_index("rad")
    core = lax.rem(rad, CORES)
    chip = lax.div(rad, CORES)
    partner = chip * CORES + (1 - core)
    me = lat * CORES + core
    other_lat = lax.rem(lat + (L - 1) * (1 - core) + core, L)

    def order(t, c):
        return t * (1 - c) + (T - 1 - t) * c

    def own_copy(q):
        return pltpu.make_async_copy(
            src.at[:, pl.ds(pl.multiple_of(core * half + q * CW, BLOCK), CW)],
            gathered.at[q, pl.ds(pl.multiple_of(rad * slab, 8), slab), :],
            own_sem.at[q],
        )

    w_copy = pltpu.make_async_copy(
        w_hbm.at[:, pl.ds(pl.multiple_of(core * half, BLOCK), half)], wv, w_sem
    )
    inputs = [
        pltpu.make_async_copy(a, b, in_sem.at[i])
        for i, (a, b) in enumerate([
            (to_hbm, to_ref), (from_hbm, from_ref), (eig_hbm, eig_ref), (nbr_hbm, nbr_ref),
            (shift_hbm.at[pl.ds(pl.multiple_of(core * NB, 8), NB), :], rows),
        ])
    ]

    def plane_peer(j):
        m = lax.rem(me + j, M)
        return m, lax.div(m, CORES), chip * CORES + lax.rem(m, CORES)

    barrier = pltpu.get_barrier_semaphore()
    for j in range(1, R):
        r = lax.rem(rad + j, R)
        pl.semaphore_signal(
            barrier, inc=1, device_id={"lat": lat, "rad": r}, device_id_type=MESH
        )
    for j in range(1, M):
        m, to_lat, to_rad = plane_peer(j)
        pl.semaphore_signal(
            barrier, inc=1, device_id={"lat": to_lat, "rad": to_rad}, device_id_type=MESH
        )
    w_copy.start()
    for copy in inputs:
        copy.start()
    for q in range(T):
        own_copy(q).start()
    pl.semaphore_wait(barrier, R - 1 + M - 1)

    pending = []

    def remote(src_ref, dst_ref, send, recv, lat_to, rad_to):
        copy = pltpu.make_async_remote_copy(
            src_ref=src_ref, dst_ref=dst_ref, send_sem=send, recv_sem=recv,
            device_id={"lat": lat_to, "rad": rad_to}, device_id_type=MESH,
        )
        copy.start()
        pending.append(copy)

    def arrived(dst_ref, send, recv):
        pltpu.make_async_remote_copy(
            src_ref=dst_ref, dst_ref=dst_ref, send_sem=send, recv_sem=recv,
            device_id={"lat": lat, "rad": partner}, device_id_type=MESH,
        ).wait_recv()

    def slot(q, r):
        return gathered.at[q, pl.ds(pl.multiple_of(r * slab, 8), slab), :]

    for t in range(T):
        for j in range(1, R):
            to = lax.rem(rad + j, R)
            to_core = lax.rem(to, CORES)
            q = order(t, to_core)
            remote(
                src.at[:, pl.ds(pl.multiple_of(to_core * half + q * CW, BLOCK), CW)],
                slot(q, rad), ag_send.at[t, j - 1], ag_recv.at[q, rad], lat, to,
            )

    w_copy.wait()
    for copy in inputs:
        copy.wait()
    row_id = lax.broadcasted_iota(jnp.int32, (A * GROUP, BLOCK), 0)

    def prepare(b, carry):
        wr[b, pl.ds((A - 1) * GROUP, GROUP), :] = jnp.zeros((GROUP, BLOCK), jnp.float32)
        wr[b, pl.ds(0, S), :] = wv[:, pl.ds(pl.multiple_of(b * BLOCK, BLOCK), BLOCK)]
        tile = wr[b, pl.ds(0, A * GROUP), :]
        placed = tile
        for c in range(1, GROUP):
            placed = jnp.where(lax.rem(row_id, GROUP) == c, pltpu.roll(tile, c, 1), placed)
        wr[b, pl.ds(0, A * GROUP), :] = placed
        diagonal = jnp.sum(tile, axis=0, keepdims=True) + rows[pl.ds(b, 1), :]
        wr[b, pl.ds(A * GROUP, GROUP), :] = jnp.broadcast_to(diagonal, (GROUP, BLOCK))
        return carry

    lax.fori_loop(0, NB, prepare, 0)
    levels = to_ref.shape[0]
    eig_t[...] = jnp.transpose(jnp.broadcast_to(eig_ref[...], (levels, levels)))

    o_at = HALO * (1 - core)
    i_at = HALO * core

    def outer_dst(c, q):
        return (1 - c) * (NB + q * CB) + c * (q * CB - NB + HALO)

    def inner_dst(c, q):
        return c * (NB + q * CB) + (1 - c) * (q * CB - NB + HALO)

    def outer_send(buf, t, send, recv):
        q = order(t, core)
        remote(
            buf.at[pl.ds(o_at + q * CB, CB)], buf.at[pl.ds(outer_dst(core, q), CB)],
            send.at[t], recv.at[t], other_lat, partner,
        )

    def outer_wait(buf, send, recv):
        for t in range(HC):
            at = outer_dst(1 - core, order(t, 1 - core))
            arrived(buf.at[pl.ds(at, CB)], send.at[t], recv.at[t])

    def inner_send(buf, base, t, send, recv):
        q = order(t, core)
        remote(
            buf.at[pl.ds(base + i_at + q * CB, CB)],
            buf.at[pl.ds(base + inner_dst(core, q), CB)],
            send.at[t - (T - HC)], recv.at[t - (T - HC)], lat, partner,
        )

    def inner_wait(buf, base, send, recv):
        for t in range(T - HC, T):
            at = inner_dst(1 - core, order(t, 1 - core))
            arrived(buf.at[pl.ds(base + at, CB)], send.at[t - (T - HC)], recv.at[t - (T - HC)])

    def spread_at(targets, value):
        for a in range(1, A):
            moved = pltpu.roll(value, BLOCK - a * GROUP, 1)
            for buf, k in targets:
                buf[a * E + k] = moved

    def spread_halo(buf, base, at):
        def step(k, carry):
            spread_at([(buf, base + at + k)], buf[base + at + k])
            return carry

        lax.fori_loop(0, HALO, step, 0)

    outer_halo = core * NB
    inner_halo = (1 - core) * NB

    def own_rows(x):
        return to_ref[pl.ds(pl.multiple_of(x * K, 8), K), :]

    def project_others(t):
        q = order(t, core)
        for j in range(1, X):
            x = lax.rem(chip + j, X)
            base = (j - 1) * A * E
            product = dot(own_rows(x), gathered[q])
            for i in range(CB):
                value = product[:, i * BLOCK:(i + 1) * BLOCK]
                modal[x, q * CB + i] = value
                others[base + i_at + q * CB + i] = value
            if t >= T - HC:
                inner_send(others, base, t, x_send.at[j - 1], x_recv.at[j - 1])
            for i in range(CB):
                spread_at(
                    [(others, base + i_at + q * CB + i)], product[:, i * BLOCK:(i + 1) * BLOCK]
                )

    for t in range(T):
        q = order(t, core)
        own_copy(q).wait()
        for j in range(1, R):
            r = lax.rem(rad + j, R)
            arrived(slot(q, r), ag_send.at[t, j - 1], ag_recv.at[q, r])
        product = dot(own_rows(chip), gathered[q])
        for i in range(CB):
            value = product[:, i * BLOCK:(i + 1) * BLOCK]
            b = q * CB + i
            outer1[o_at + b] = value
            inner1[i_at + b] = value
            modal[chip, b] = value
        if t < HC:
            outer_send(outer1, t, o1_send, o1_recv)
        if t >= T - HC:
            inner_send(inner1, 0, t, i1_send, i1_recv)
        for i in range(CB):
            b = q * CB + i
            spread_at(
                [(outer1, o_at + b), (inner1, i_at + b)], product[:, i * BLOCK:(i + 1) * BLOCK]
            )
        if t < T - 1:
            project_others(t)
        if t == T - 2:
            outer_wait(outer1, o1_send, o1_recv)
            spread_halo(outer1, 0, outer_halo)

    def operate(buf, base, x, b, field):
        total = None
        for c in range(GROUP):
            inner = None
            for a in range(A):
                s = a * GROUP + c
                if s < S:
                    n = nbr_ref[s, core * NB + b]
                    term = buf[base + a * E + b + n] * wr[b, pl.ds(s, 1), :]
                    inner = term if inner is None else inner + term
            if inner is not None:
                moved = inner if c == 0 else pltpu.roll(inner, BLOCK - c, 1)
                total = moved if total is None else total + moved
        eig = eig_t[pl.ds(pl.multiple_of(x * K, 8), K), :]
        return (wr[b, pl.ds(A * GROUP, 1), :] + eig) * field - total

    def first_pass(buf, at):
        def step(b, carry):
            field = modal[chip, b]
            value = operate(buf, at, chip, b, field)
            outer2[o_at + b] = value
            inner2[i_at + b] = value
            image[chip, b] = value
            return (carry[0] + field * field, carry[1] + value * value)

        return step

    zero = jnp.zeros((K, BLOCK), jnp.float32)
    sums = (zero, zero)
    for t in range(T):
        q = order(t, core)
        if t == T // 2:
            inner_wait(inner1, 0, i1_send, i1_recv)
            spread_halo(inner1, 0, inner_halo)
        step = first_pass(outer1, o_at) if t < T // 2 else first_pass(inner1, i_at)
        sums = lax.fori_loop(q * CB, (q + 1) * CB, step, sums)
        if t < HC:
            outer_send(outer2, t, o2_send, o2_recv)
        if t < T // 2:
            for j in range(1, X):
                to = lax.rem(chip + j, X)
                remote(
                    image.at[chip, pl.ds(q * CB, CB)], image.at[chip, pl.ds(q * CB, CB)],
                    im_send.at[t, j - 1], im_recv.at[q, chip], lat, to * CORES + core,
                )
        if t >= T - HC:
            inner_send(inner2, 0, t, i2_send, i2_recv)

    ones = jnp.ones((8, BLOCK), jnp.float32)

    def lanes(values):
        line = lax.dot_general(
            ones, values, (((1,), (1,)), ((), ())), precision=HIGHEST,
            preferred_element_type=jnp.float32,
        )
        width = line.shape[1]
        if width < BLOCK:
            line = jnp.concatenate(
                [line, jnp.zeros((8, BLOCK - width), jnp.float32)], axis=1
            )
        return line[0:1]

    def plane_send(buf, send, recv):
        for j in range(1, M):
            m, to_lat, to_rad = plane_peer(j)
            remote(buf.at[me], buf.at[me], send.at[j - 1], recv.at[me], to_lat, to_rad)

    def plane_sum(buf, send, recv):
        for j in range(1, M):
            m = lax.rem(me + j, M)
            arrived(buf.at[m], send.at[j - 1], recv.at[m])
        total = buf[0]
        for m in range(1, M):
            total = total + buf[m]
        return total

    s1[me] = lanes(jnp.concatenate(sums, axis=0))
    plane_send(s1, s1_send, s1_recv)
    project_others(T - 1)

    inside = (NB // 2) * (1 - core)
    for j in range(1, X):
        x = lax.rem(chip + j, X)
        base = (j - 1) * A * E
        inner_wait(others, base, x_send.at[j - 1], x_recv.at[j - 1])
        spread_halo(others, base, inner_halo)
    for j in range(1, X):
        x = lax.rem(chip + j, X)
        base = (j - 1) * A * E

        def others_pass(b, carry, x=x, base=base):
            image[x, b] = operate(others, base + i_at, x, b, modal[x, b])
            return carry

        lax.fori_loop(inside, inside + NB // 2, others_pass, 0)

    mine = jnp.concatenate(
        [
            from_ref[pl.ds(pl.multiple_of(rad * slab, 8), slab), :],
            from_ref[pl.ds(pl.multiple_of(partner * slab, 8), slab), :],
        ],
        axis=0,
    )

    def columns(q):
        return out.at[:, pl.ds(pl.multiple_of(core * half + q * CW, BLOCK), CW)]

    def their_columns(q):
        return out.at[:, pl.ds(pl.multiple_of((1 - core) * half + q * CW, BLOCK), CW)]

    def finish(t):
        q = order(t, core)
        if t < T // 2:
            for j in range(1, X):
                x = lax.rem(chip + j, X)
                arrived(image.at[x, pl.ds(q * CB, CB)], im_send.at[t, j - 1], im_recv.at[q, x])
        blocks = []
        for i in range(CB):
            b = q * CB + i
            blocks.append(
                jnp.concatenate(
                    [coef[x, 0] * modal[x, b] + coef[x, 1] * image[x, b] for x in range(X)], axis=0
                )
            )
        product = dot(mine, jnp.concatenate(blocks, axis=1))
        part[q, 0] = product[0:slab]
        part[q, 1] = product[slab:K]
        remote(part.at[q, 1], columns(q), out_send.at[q], out_recv.at[q], lat, partner)
        pltpu.make_async_copy(part.at[q, 0], columns(q), out_sem.at[q]).start()

    def second_pass(buf, at):
        def step(b, carry):
            twice[b] = operate(buf, at, chip, b, image[chip, b])
            return carry

        return step

    def spread_own(b, carry):
        spread_at([(outer2, o_at + b), (inner2, i_at + b)], image[chip, b])
        return carry

    def residual(b, carry):
        final = modal[chip, b] - (coef[chip, 0] * image[chip, b] + coef[chip, 1] * twice[b])
        return carry + final * final

    lax.fori_loop(0, NB, spread_own, 0)
    inner_wait(inner2, 0, i2_send, i2_recv)
    spread_halo(inner2, 0, inner_halo)
    s2[chip] = plane_sum(s1, s1_send, s1_recv)
    for j in range(1, X):
        x = lax.rem(chip + j, X)
        remote(
            s2.at[chip], s2.at[chip], s2_send.at[j - 1], s2_recv.at[chip], lat, x * CORES + core
        )

    lax.fori_loop(inside, inside + NB // 2, second_pass(inner2, i_at), 0)
    outer_wait(outer2, o2_send, o2_recv)
    spread_halo(outer2, 0, outer_halo)
    outside = (NB // 2) * core
    lax.fori_loop(outside, outside + NB // 2, second_pass(outer2, o_at), 0)

    for j in range(1, X):
        x = lax.rem(chip + j, X)
        arrived(s2.at[x], s2_send.at[j - 1], s2_recv.at[x])
    for x in range(X):
        column = jnp.transpose(jnp.broadcast_to(s2[x], (BLOCK, BLOCK)))
        base, power = column[0:K], column[K:2 * K]
        upper = 1.5 * jnp.sqrt(power / (base + 1e-06))
        lower = upper * 0.125
        center = (upper + lower) * 0.5
        half_width = (upper - lower) * 0.5
        sigma = center / half_width
        rho_zero = 1.0 / sigma
        rho_one = 1.0 / (2.0 * sigma - rho_zero)
        second = 2.0 * rho_one / half_width
        coef[x, 0] = (1.0 + rho_one * rho_zero) / center + second
        coef[x, 1] = -second / center

    s3[me] = lanes(lax.fori_loop(0, NB, residual, zero))
    plane_send(s3, s3_send, s3_recv)
    for t in range(T // 2, T):
        finish(t)
    for t in range(T // 2):
        finish(t)

    norm = jnp.sqrt(plane_sum(s3, s3_send, s3_recv) / (s2[chip] + 1e-06))
    res_ref[...] = jnp.where(core == 0, norm[:, 0:slab], norm[:, slab:2 * slab])

    for q in range(T):
        pltpu.make_async_copy(part.at[q, 0], columns(q), out_sem.at[q]).wait()
        arrived(their_columns(q), out_send.at[q], out_recv.at[q])
    for copy in pending:
        copy.wait_send()


def on_device(L, R, source, to_modes, from_modes, eigenvalue, shifts, weights, neighbors):
    slab, nodes = source.shape
    S = weights.shape[0]
    levels = to_modes.shape[0]
    T, X, K = CHUNKS, R // CORES, slab * CORES
    half = nodes // CORES
    NB = half // BLOCK
    CW = half // T
    E = NB + HALO
    A = -(-S // GROUP)
    M = L * CORES
    HC = HALO // (NB // T)
    f32 = jnp.float32

    def window(count):
        return pltpu.VMEM((count * A * E, K, BLOCK), f32)

    dma = pltpu.SemaphoreType.DMA
    vmem = pl.BlockSpec(memory_space=pltpu.VMEM)
    hbm = pl.BlockSpec(memory_space=pltpu.HBM)
    smoothed, norm = pl.pallas_call(
        functools.partial(kernel, L, R, S),
        name="smoother",
        out_shape=(
            pltpu.VMEM((slab, nodes), f32),
            jax.ShapeDtypeStruct((1, slab), f32),
        ),
        in_specs=[hbm] * 7,
        out_specs=(vmem, vmem),
        scratch_shapes=[
            pltpu.VMEM((T, levels, CW), f32),
            pltpu.VMEM((S, half), f32),
            pltpu.VMEM((NB, (A + 1) * GROUP, BLOCK), f32),
            window(1), window(1), window(1), window(1), window(X - 1),
            pltpu.VMEM((X, NB, K, BLOCK), f32),
            pltpu.VMEM((X, NB, K, BLOCK), f32),
            pltpu.VMEM((NB, K, BLOCK), f32),
            pltpu.VMEM((levels, levels), f32),
            pltpu.VMEM((X, 2, K, BLOCK), f32),
            pltpu.VMEM((T, 2, slab, CW), f32),
            pltpu.VMEM((NB, BLOCK), f32),
            pltpu.VMEM((M, 1, BLOCK), f32),
            pltpu.VMEM((X, 1, BLOCK), f32),
            pltpu.VMEM((M, 1, BLOCK), f32),
            pltpu.VMEM((levels, levels), f32),
            pltpu.VMEM((levels, levels), f32),
            pltpu.VMEM((1, levels), f32),
            pltpu.SMEM(neighbors.shape, jnp.int32),
            dma((5,)), dma((T,)), dma(()),
            dma((T, R - 1)), dma((T, R)),
            *[dma((HC,)) for _ in range(8)],
            dma((X - 1, HC)), dma((X - 1, HC)),
            dma((T, X - 1)), dma((T, X)),
            dma((M - 1,)), dma((M,)), dma((X - 1,)), dma((X,)),
            dma((M - 1,)), dma((M,)),
            dma((T,)), dma((T,)), dma((T,)),
        ],
        compiler_params=pltpu.CompilerParams(
            collective_id=0, has_side_effects=True, vmem_limit_bytes=67043328 - 4 * slab * nodes - 4096
        ),
    )(
        source, weights, to_modes, from_modes, eigenvalue.reshape(1, levels),
        shifts.reshape(nodes // BLOCK, BLOCK), neighbors,
    )
    return smoothed, norm.reshape(slab)


def solution(mesh):
    return jax.shard_map(
        functools.partial(on_device, mesh.shape["lat"], mesh.shape["rad"]),
        mesh=mesh,
        in_specs=(P("rad", "lat"), P(), P(), P(), P("lat"), P(None, "lat"), P(None, "lat")),
        out_specs=(P("rad", "lat"), P("rad")),
        check_vma=False,
    )
```

profile of v0, /device:TPU:0, one launch (start us, length us, event | category | flops | bytes accessed | tf_op | source)
XLA Modules:
  0.0 41.0 jit_solution(14939548042970591373)
XLA Ops:
  0.6 38.5 %smoother.1 = (f32[32,4096]{1,0:T(8,128)S(1)}, f32[1,32]{1,0:T(1,128)}) custom-call(f32[32,4096]{1,0:T(8,128)} %src.1, f32[31,4096]{1,0:T(8,128)} %w_hbm.1, f32[128,128]{1,0:T(8,128)} %to_hbm.1, f32[128,128]{1,0:T(8,128)} %from_hbm.1, f32[1,128]{1,0:T(1,128)} %bitcast.4, f32[32,128]{1,0:T(8,128)} %bitcast.3, s32[31,32]{1,0:T(8,128)} %nbr_hbm.1), custom_call_target="tpu_custom_call" | custom-call | tf_op jit(solution)/shard_map/smoother/pallas_call | solution.py:460
  39.1 0.8 %copy.11 = f32[32,4096]{1,0:T(8,128)} copy(f32[32,4096]{1,0:T(8,128)S(1)} %get-tuple-element.6) | data formatting | bytes 1048576
  39.9 0.0 copy-start
  39.9 0.6 %copy-done = f32[1,32]{1,0:T(1,128)S(1)} copy-done((f32[1,32]{1,0:T(1,128)S(1)}, f32[1,32]{1,0:T(1,128)}, u32[]{:S(2)}) %copy-start) | copy-done | bytes 152
  40.5 0.5 %copy.12 = f32[32]{0:T(128)} copy(f32[32]{0:T(128)S(1)} %bitcast.5) | data formatting | bytes 256
Async XLA Ops:
  39.9 0.6 %copy-start = (f32[1,32]{1,0:T(1,128)S(1)}, f32[1,32]{1,0:T(1,128)}, u32[]{:S(2)}) copy-start(f32[1,32]{1,0:T(1,128)} %get-tuple-element.5) | copy-start | bytes 388
where the time goes:
time: 41.2 us; the launch traced here: 41 us
  Pallas kernels  38.5 us (93%)
  local copies, waits for them, and re-layouts  1.93 us (5%)
  between operations  0.64 us (2%)
    pallas_call x1, Pallas kernels, on_device(): pl.pallas_call(functools.partial(kernel, L, R, S), name='smoother', out_s...  38.5 us
    unnamed x4, local copies, waits for them, and re-layouts  1.93 us

commit v1 on v0

--- a/solution.py
+++ b/solution.py
@@ -1,4 +1,5 @@
 import functools
+import math
 
 import jax
 import jax.numpy as jnp
@@ -11,6 +12,7 @@
 HALO = 8
 CHUNKS = 4
 GROUP = 8
+UNROLL = 4
 CORES = 2
 HIGHEST = lax.Precision.HIGHEST
 MESH = pl.DeviceIdType.MESH
@@ -18,6 +20,19 @@
 
 def dot(a, b):
     return jnp.dot(a, b, precision=HIGHEST, preferred_element_type=jnp.float32)
+
+
+def repeat(count, step, carry):
+    width = math.gcd(count, UNROLL)
+
+    def trip(n, carry):
+        for j in range(width):
+            carry = step(n * width + j, carry)
+        return carry
+
+    if count == width:
+        return trip(0, carry)
+    return lax.fori_loop(0, count // width, trip, carry)
 
 
 def kernel(
@@ -26,10 +41,7 @@
     out, res_ref,
     gathered, wv, wr, outer1, inner1, outer2, inner2, others, modal, image, twice, eig_t, coef, part,
     rows, s1, s2, s3, to_ref, from_ref, eig_ref, nbr_ref,
-    in_sem, own_sem, w_sem, ag_send, ag_recv,
-    o1_send, o1_recv, i1_send, i1_recv, o2_send, o2_recv, i2_send, i2_recv, x_send, x_recv,
-    im_send, im_recv, s1_send, s1_recv, s2_send, s2_recv, s3_send, s3_recv,
-    out_send, out_recv, out_sem,
+    in_sem, own_sem, w_sem, ag_recv, im_recv, x_recv, send_sem, recv_sem, out_sem,
 ):
     T = CHUNKS
     X = R // CORES
@@ -58,7 +70,7 @@
         return pltpu.make_async_copy(
             src.at[:, pl.ds(pl.multiple_of(core * half + q * CW, BLOCK), CW)],
             gathered.at[q, pl.ds(pl.multiple_of(rad * slab, 8), slab), :],
-            own_sem.at[q],
+            own_sem,
         )
 
     w_copy = pltpu.make_async_copy(
@@ -94,21 +106,22 @@
         own_copy(q).start()
     pl.semaphore_wait(barrier, R - 1 + M - 1)
 
-    pending = []
-
-    def remote(src_ref, dst_ref, send, recv, lat_to, rad_to):
-        copy = pltpu.make_async_remote_copy(
-            src_ref=src_ref, dst_ref=dst_ref, send_sem=send, recv_sem=recv,
+    AG, O1, I1, O2, I2, OT, IM, S1, S2, S3, OUT = range(11)
+
+    def remote(src_ref, dst_ref, kind, recv, lat_to, rad_to):
+        pltpu.make_async_remote_copy(
+            src_ref=src_ref, dst_ref=dst_ref, send_sem=send_sem.at[kind], recv_sem=recv,
             device_id={"lat": lat_to, "rad": rad_to}, device_id_type=MESH,
-        )
-        copy.start()
-        pending.append(copy)
-
-    def arrived(dst_ref, send, recv):
-        pltpu.make_async_remote_copy(
-            src_ref=dst_ref, dst_ref=dst_ref, send_sem=send, recv_sem=recv,
+        ).start()
+
+    def whole(ref, kind, recv):
+        return pltpu.make_async_remote_copy(
+            src_ref=ref, dst_ref=ref, send_sem=send_sem.at[kind], recv_sem=recv,
             device_id={"lat": lat, "rad": partner}, device_id_type=MESH,
-        ).wait_recv()
+        )
+
+    def arrived(ref, recv):
+        whole(ref, AG, recv).wait_recv()
 
     def slot(q, r):
         return gathered.at[q, pl.ds(pl.multiple_of(r * slab, 8), slab), :]
@@ -120,7 +133,7 @@
             q = order(t, to_core)
             remote(
                 src.at[:, pl.ds(pl.multiple_of(to_core * half + q * CW, BLOCK), CW)],
-                slot(q, rad), ag_send.at[t, j - 1], ag_recv.at[q, rad], lat, to,
+                slot(q, rad), AG, ag_recv.at[q], lat, to,
             )
 
     w_copy.wait()
@@ -140,7 +153,7 @@
         wr[b, pl.ds(A * GROUP, GROUP), :] = jnp.broadcast_to(diagonal, (GROUP, BLOCK))
         return carry
 
-    lax.fori_loop(0, NB, prepare, 0)
+    repeat(NB, prepare, 0)
     levels = to_ref.shape[0]
     eig_t[...] = jnp.transpose(jnp.broadcast_to(eig_ref[...], (levels, levels)))
 
@@ -153,30 +166,29 @@
     def inner_dst(c, q):
         return c * (NB + q * CB) + (1 - c) * (q * CB - NB + HALO)
 
-    def outer_send(buf, t, send, recv):
+    outer_halo = core * NB
+    inner_halo = (1 - core) * NB
+
+    def outer_send(buf, t, kind):
         q = order(t, core)
         remote(
             buf.at[pl.ds(o_at + q * CB, CB)], buf.at[pl.ds(outer_dst(core, q), CB)],
-            send.at[t], recv.at[t], other_lat, partner,
-        )
-
-    def outer_wait(buf, send, recv):
-        for t in range(HC):
-            at = outer_dst(1 - core, order(t, 1 - core))
-            arrived(buf.at[pl.ds(at, CB)], send.at[t], recv.at[t])
-
-    def inner_send(buf, base, t, send, recv):
+            kind, recv_sem.at[kind], other_lat, partner,
+        )
+
+    def outer_wait(buf, kind):
+        arrived(buf.at[pl.ds(outer_halo, HALO)], recv_sem.at[kind])
+
+    def inner_send(buf, base, t, kind, recv):
         q = order(t, core)
         remote(
             buf.at[pl.ds(base + i_at + q * CB, CB)],
             buf.at[pl.ds(base + inner_dst(core, q), CB)],
-            send.at[t - (T - HC)], recv.at[t - (T - HC)], lat, partner,
-        )
-
-    def inner_wait(buf, base, send, recv):
-        for t in range(T - HC, T):
-            at = inner_dst(1 - core, order(t, 1 - core))
-            arrived(buf.at[pl.ds(base + at, CB)], send.at[t - (T - HC)], recv.at[t - (T - HC)])
+            kind, recv, lat, partner,
+        )
+
+    def inner_wait(buf, base, recv):
+        arrived(buf.at[pl.ds(base + inner_halo, HALO)], recv)
 
     def spread_at(targets, value):
         for a in range(1, A):
@@ -189,10 +201,7 @@
             spread_at([(buf, base + at + k)], buf[base + at + k])
             return carry
 
-        lax.fori_loop(0, HALO, step, 0)
-
-    outer_halo = core * NB
-    inner_halo = (1 - core) * NB
+        repeat(HALO, step, 0)
 
     def own_rows(x):
         return to_ref[pl.ds(pl.multiple_of(x * K, 8), K), :]
@@ -208,39 +217,11 @@
                 modal[x, q * CB + i] = value
                 others[base + i_at + q * CB + i] = value
             if t >= T - HC:
-                inner_send(others, base, t, x_send.at[j - 1], x_recv.at[j - 1])
+                inner_send(others, base, t, OT, x_recv.at[j - 1])
             for i in range(CB):
                 spread_at(
                     [(others, base + i_at + q * CB + i)], product[:, i * BLOCK:(i + 1) * BLOCK]
                 )
-
-    for t in range(T):
-        q = order(t, core)
-        own_copy(q).wait()
-        for j in range(1, R):
-            r = lax.rem(rad + j, R)
-            arrived(slot(q, r), ag_send.at[t, j - 1], ag_recv.at[q, r])
-        product = dot(own_rows(chip), gathered[q])
-        for i in range(CB):
-            value = product[:, i * BLOCK:(i + 1) * BLOCK]
-            b = q * CB + i
-            outer1[o_at + b] = value
-            inner1[i_at + b] = value
-            modal[chip, b] = value
-        if t < HC:
-            outer_send(outer1, t, o1_send, o1_recv)
-        if t >= T - HC:
-            inner_send(inner1, 0, t, i1_send, i1_recv)
-        for i in range(CB):
-            b = q * CB + i
-            spread_at(
-                [(outer1, o_at + b), (inner1, i_at + b)], product[:, i * BLOCK:(i + 1) * BLOCK]
-            )
-        if t < T - 1:
-            project_others(t)
-        if t == T - 2:
-            outer_wait(outer1, o1_send, o1_recv)
-            spread_halo(outer1, 0, outer_halo)
 
     def operate(buf, base, x, b, field):
         total = None
@@ -270,25 +251,58 @@
         return step
 
     zero = jnp.zeros((K, BLOCK), jnp.float32)
-    sums = (zero, zero)
-    for t in range(T):
+
+    def first(t, buf, at, sums):
         q = order(t, core)
-        if t == T // 2:
-            inner_wait(inner1, 0, i1_send, i1_recv)
-            spread_halo(inner1, 0, inner_halo)
-        step = first_pass(outer1, o_at) if t < T // 2 else first_pass(inner1, i_at)
-        sums = lax.fori_loop(q * CB, (q + 1) * CB, step, sums)
+        step = first_pass(buf, at)
+        sums = repeat(CB, lambda i, carry: step(q * CB + i, carry), sums)
         if t < HC:
-            outer_send(outer2, t, o2_send, o2_recv)
-        if t < T // 2:
+            outer_send(outer2, t, O2)
             for j in range(1, X):
                 to = lax.rem(chip + j, X)
                 remote(
                     image.at[chip, pl.ds(q * CB, CB)], image.at[chip, pl.ds(q * CB, CB)],
-                    im_send.at[t, j - 1], im_recv.at[q, chip], lat, to * CORES + core,
+                    IM, im_recv.at[q], lat, to * CORES + core,
                 )
         if t >= T - HC:
-            inner_send(inner2, 0, t, i2_send, i2_recv)
+            inner_send(inner2, 0, t, I2, recv_sem.at[I2])
+        return sums
+
+    sums = (zero, zero)
+    for t in range(T):
+        q = order(t, core)
+        if t == 0:
+            mine_at = gathered.at[:, pl.ds(pl.multiple_of(rad * slab, 8), slab), :]
+            pltpu.make_async_copy(mine_at, mine_at, own_sem).wait()
+        arrived(gathered.at[q, pl.ds(0, (R - 1) * slab), :], ag_recv.at[q])
+        product = dot(own_rows(chip), gathered[q])
+        for i in range(CB):
+            value = product[:, i * BLOCK:(i + 1) * BLOCK]
+            b = q * CB + i
+            outer1[o_at + b] = value
+            inner1[i_at + b] = value
+            modal[chip, b] = value
+        if t < HC:
+            outer_send(outer1, t, O1)
+        if t >= T - HC:
+            inner_send(inner1, 0, t, I1, recv_sem.at[I1])
+        for i in range(CB):
+            b = q * CB + i
+            spread_at(
+                [(outer1, o_at + b), (inner1, i_at + b)], product[:, i * BLOCK:(i + 1) * BLOCK]
+            )
+        if t < T - 1:
+            project_others(t)
+        if t == HC:
+            outer_wait(outer1, O1)
+            spread_halo(outer1, 0, outer_halo)
+        if t >= HC:
+            sums = first(t - HC, outer1, o_at, sums)
+    project_others(T - 1)
+    inner_wait(inner1, 0, recv_sem.at[I1])
+    spread_halo(inner1, 0, inner_halo)
+    for t in range(T - HC, T):
+        sums = first(t, inner1, i_at, sums)
 
     ones = jnp.ones((8, BLOCK), jnp.float32)
 
@@ -304,39 +318,37 @@
             )
         return line[0:1]
 
-    def plane_send(buf, send, recv):
+    def plane_send(buf, kind):
         for j in range(1, M):
             m, to_lat, to_rad = plane_peer(j)
-            remote(buf.at[me], buf.at[me], send.at[j - 1], recv.at[me], to_lat, to_rad)
-
-    def plane_sum(buf, send, recv):
-        for j in range(1, M):
-            m = lax.rem(me + j, M)
-            arrived(buf.at[m], send.at[j - 1], recv.at[m])
+            remote(buf.at[me], buf.at[me], kind, recv_sem.at[kind], to_lat, to_rad)
+
+    def plane_sum(buf, kind):
+        arrived(buf.at[pl.ds(0, M - 1)], recv_sem.at[kind])
         total = buf[0]
         for m in range(1, M):
             total = total + buf[m]
         return total
 
     s1[me] = lanes(jnp.concatenate(sums, axis=0))
-    plane_send(s1, s1_send, s1_recv)
-    project_others(T - 1)
+    plane_send(s1, S1)
 
     inside = (NB // 2) * (1 - core)
     for j in range(1, X):
         x = lax.rem(chip + j, X)
         base = (j - 1) * A * E
-        inner_wait(others, base, x_send.at[j - 1], x_recv.at[j - 1])
+        inner_wait(others, base, x_recv.at[j - 1])
         spread_halo(others, base, inner_halo)
     for j in range(1, X):
         x = lax.rem(chip + j, X)
         base = (j - 1) * A * E
 
-        def others_pass(b, carry, x=x, base=base):
+        def others_pass(i, carry, x=x, base=base):
+            b = inside + i
             image[x, b] = operate(others, base + i_at, x, b, modal[x, b])
             return carry
 
-        lax.fori_loop(inside, inside + NB // 2, others_pass, 0)
+        repeat(NB // 2, others_pass, 0)
 
     mine = jnp.concatenate(
         [
@@ -349,15 +361,16 @@
     def columns(q):
         return out.at[:, pl.ds(pl.multiple_of(core * half + q * CW, BLOCK), CW)]
 
-    def their_columns(q):
-        return out.at[:, pl.ds(pl.multiple_of((1 - core) * half + q * CW, BLOCK), CW)]
+    def columns_of(c):
+        return out.at[:, pl.ds(c * half, half)]
 
     def finish(t):
         q = order(t, core)
-        if t < T // 2:
+        if t < HC:
             for j in range(1, X):
                 x = lax.rem(chip + j, X)
-                arrived(image.at[x, pl.ds(q * CB, CB)], im_send.at[t, j - 1], im_recv.at[q, x])
+                if j == 1:
+                    arrived(image.at[pl.ds(0, X - 1), pl.ds(q * CB, CB)], im_recv.at[q])
         blocks = []
         for i in range(CB):
             b = q * CB + i
@@ -369,43 +382,43 @@
         product = dot(mine, jnp.concatenate(blocks, axis=1))
         part[q, 0] = product[0:slab]
         part[q, 1] = product[slab:K]
-        remote(part.at[q, 1], columns(q), out_send.at[q], out_recv.at[q], lat, partner)
-        pltpu.make_async_copy(part.at[q, 0], columns(q), out_sem.at[q]).start()
-
-    def second_pass(buf, at):
-        def step(b, carry):
-            twice[b] = operate(buf, at, chip, b, image[chip, b])
-            return carry
-
-        return step
+        remote(part.at[q, 1], columns(q), OUT, recv_sem.at[OUT], lat, partner)
+        pltpu.make_async_copy(part.at[q, 0], columns(q), out_sem).start()
 
     def spread_own(b, carry):
         spread_at([(outer2, o_at + b), (inner2, i_at + b)], image[chip, b])
         return carry
 
-    def residual(b, carry):
-        final = modal[chip, b] - (coef[chip, 0] * image[chip, b] + coef[chip, 1] * twice[b])
+    def residual(b, value, carry):
+        final = modal[chip, b] - (coef[chip, 0] * image[chip, b] + coef[chip, 1] * value)
         return carry + final * final
 
-    lax.fori_loop(0, NB, spread_own, 0)
-    inner_wait(inner2, 0, i2_send, i2_recv)
+    def second_inside(i, carry):
+        b = inside + i
+        twice[b] = operate(inner2, i_at, chip, b, image[chip, b])
+        return carry
+
+    def residual_inside(i, carry):
+        b = inside + i
+        return residual(b, twice[b], carry)
+
+    outside = (NB // 2) * core
+
+    def second_outside(i, carry):
+        b = outside + i
+        return residual(b, operate(outer2, o_at, chip, b, image[chip, b]), carry)
+
+    repeat(NB, spread_own, 0)
+    inner_wait(inner2, 0, recv_sem.at[I2])
     spread_halo(inner2, 0, inner_halo)
-    s2[chip] = plane_sum(s1, s1_send, s1_recv)
+    s2[chip] = plane_sum(s1, S1)
     for j in range(1, X):
         x = lax.rem(chip + j, X)
-        remote(
-            s2.at[chip], s2.at[chip], s2_send.at[j - 1], s2_recv.at[chip], lat, x * CORES + core
-        )
-
-    lax.fori_loop(inside, inside + NB // 2, second_pass(inner2, i_at), 0)
-    outer_wait(outer2, o2_send, o2_recv)
-    spread_halo(outer2, 0, outer_halo)
-    outside = (NB // 2) * core
-    lax.fori_loop(outside, outside + NB // 2, second_pass(outer2, o_at), 0)
-
-    for j in range(1, X):
-        x = lax.rem(chip + j, X)
-        arrived(s2.at[x], s2_send.at[j - 1], s2_recv.at[x])
+        remote(s2.at[chip], s2.at[chip], S2, recv_sem.at[S2], lat, x * CORES + core)
+
+    repeat(NB // 2, second_inside, 0)
+
+    arrived(s2.at[pl.ds(0, X - 1)], recv_sem.at[S2])
     for x in range(X):
         column = jnp.transpose(jnp.broadcast_to(s2[x], (BLOCK, BLOCK)))
         base, power = column[0:K], column[K:2 * K]
@@ -420,21 +433,30 @@
         coef[x, 0] = (1.0 + rho_one * rho_zero) / center + second
         coef[x, 1] = -second / center
 
-    s3[me] = lanes(lax.fori_loop(0, NB, residual, zero))
-    plane_send(s3, s3_send, s3_recv)
-    for t in range(T // 2, T):
+    final = repeat(NB // 2, residual_inside, zero)
+    for t in range(HC, T):
         finish(t)
-    for t in range(T // 2):
+    outer_wait(outer2, O2)
+    spread_halo(outer2, 0, outer_halo)
+    s3[me] = lanes(repeat(NB // 2, second_outside, final))
+    plane_send(s3, S3)
+    for t in range(HC):
         finish(t)
 
-    norm = jnp.sqrt(plane_sum(s3, s3_send, s3_recv) / (s2[chip] + 1e-06))
+    norm = jnp.sqrt(plane_sum(s3, S3) / (s2[chip] + 1e-06))
     res_ref[...] = jnp.where(core == 0, norm[:, 0:slab], norm[:, slab:2 * slab])
 
-    for q in range(T):
-        pltpu.make_async_copy(part.at[q, 0], columns(q), out_sem.at[q]).wait()
-        arrived(their_columns(q), out_send.at[q], out_recv.at[q])
-    for copy in pending:
-        copy.wait_send()
+    everything = columns_of(0)
+    pltpu.make_async_copy(everything, everything, out_sem).wait()
+    whole(columns_of(0), OUT, recv_sem.at[OUT]).wait()
+    whole(gathered.at[:, pl.ds(0, (R - 1) * slab), :], AG, ag_recv.at[0]).wait_send()
+    for kind in (O1, I1, O2, I2):
+        whole(outer1.at[pl.ds(0, HALO)], kind, recv_sem.at[kind]).wait_send()
+    whole(others.at[pl.ds(0, (X - 1) * HALO)], OT, recv_sem.at[OT]).wait_send()
+    whole(image.at[pl.ds(0, X - 1), pl.ds(0, HALO)], IM, recv_sem.at[IM]).wait_send()
+    for buf, kind in ((s1, S1), (s3, S3)):
+        whole(buf.at[pl.ds(0, M - 1)], kind, recv_sem.at[kind]).wait_send()
+    whole(s2.at[pl.ds(0, X - 1)], S2, recv_sem.at[S2]).wait_send()
 
 
 def on_device(L, R, source, to_modes, from_modes, eigenvalue, shifts, weights, neighbors):
@@ -448,7 +470,6 @@
     E = NB + HALO
     A = -(-S // GROUP)
     M = L * CORES
-    HC = HALO // (NB // T)
     f32 = jnp.float32
 
     def window(count):
@@ -462,7 +483,7 @@
         name="smoother",
         out_shape=(
             pltpu.VMEM((slab, nodes), f32),
-            jax.ShapeDtypeStruct((1, slab), f32),
+            pltpu.VMEM((1, slab), f32),
         ),
         in_specs=[hbm] * 7,
         out_specs=(vmem, vmem),
@@ -485,14 +506,9 @@
             pltpu.VMEM((levels, levels), f32),
             pltpu.VMEM((1, levels), f32),
             pltpu.SMEM(neighbors.shape, jnp.int32),
-            dma((5,)), dma((T,)), dma(()),
-            dma((T, R - 1)), dma((T, R)),
-            *[dma((HC,)) for _ in range(8)],
-            dma((X - 1, HC)), dma((X - 1, HC)),
-            dma((T, X - 1)), dma((T, X)),
-            dma((M - 1,)), dma((M,)), dma((X - 1,)), dma((X,)),
-            dma((M - 1,)), dma((M,)),
-            dma((T,)), dma((T,)), dma((T,)),
+            dma((5,)), dma(()), dma(()),
+            dma((T,)), dma((T,)), dma((X - 1,)),
+            dma((11,)), dma((11,)), dma(()),
         ],
         compiler_params=pltpu.CompilerParams(
             collective_id=0, has_side_effects=True, vmem_limit_bytes=67043328 - 4 * slab * nodes - 4096

time: 41.2 us -> 37.3 us (0.905)
  Pallas kernels: 38.5 us -> 35.2 us
  local copies, waits for them, and re-layouts: 1.93 us -> 1.31 us
    pallas_call x1, Pallas kernels: 38.5 us -> 35.2 us  [on_device(): pl.pallas_call(functools.partial(kernel, L, R, S), name='smoother', out_s...]
    unnamed x4 -> x2, local copies, waits for them, and re-layouts: 1.93 us -> 1.31 us
where the time goes in v1:
time: 37.3 us; the launch traced here: 37.2 us
  Pallas kernels  35.2 us (94%)
  local copies, waits for them, and re-layouts  1.31 us (4%)
  between operations  0.64 us (2%)
    pallas_call x1, Pallas kernels, on_device(): pl.pallas_call(functools.partial(kernel, L, R, S), name='smoother', out_s...  35.2 us
    unnamed x2, local copies, waits for them, and re-layouts  1.31 us

profile of v1, /device:TPU:0, one launch (start us, length us, event | category | flops | bytes accessed | tf_op | source)
XLA Modules:
  0.0 37.2 jit_solution(10417193531824553830)
XLA Ops:
  0.6 35.2 %smoother.1 = (f32[32,4096]{1,0:T(8,128)S(1)}, f32[1,32]{1,0:T(1,128)S(1)}) custom-call(f32[32,4096]{1,0:T(8,128)} %src.1, f32[31,4096]{1,0:T(8,128)} %w_hbm.1, f32[128,128]{1,0:T(8,128)} %to_hbm.1, f32[128,128]{1,0:T(8,128)} %from_hbm.1, f32[1,128]{1,0:T(1,128)} %bitcast.5, f32[32,128]{1,0:T(8,128)} %bitcast.4, s32[31,32]{1,0:T(8,128)} %nbr_hbm.1), custom_call_target="tpu_custom_call" | custom-call | tf_op jit(solution)/shard_map/smoother/pallas_call | solution.py:481
  35.9 0.8 %copy.11 = f32[32,4096]{1,0:T(8,128)} copy(f32[32,4096]{1,0:T(8,128)S(1)} %get-tuple-element.6) | data formatting | bytes 1048576
  36.7 0.5 %copy.12 = f32[32]{0:T(128)} copy(f32[32]{0:T(128)S(1)} %bitcast.3) | data formatting | bytes 256

commit v2 on v1

--- a/solution.py
+++ b/solution.py
@@ -13,6 +13,7 @@
 CHUNKS = 4
 GROUP = 8
 UNROLL = 4
+STEP = 2
 CORES = 2
 HIGHEST = lax.Precision.HIGHEST
 MESH = pl.DeviceIdType.MESH
@@ -41,7 +42,7 @@
     out, res_ref,
     gathered, wv, wr, outer1, inner1, outer2, inner2, others, modal, image, twice, eig_t, coef, part,
     rows, s1, s2, s3, to_ref, from_ref, eig_ref, nbr_ref,
-    in_sem, own_sem, w_sem, ag_recv, im_recv, x_recv, send_sem, recv_sem, out_sem,
+    in_sem, own_sem, w_sem, ag_recv, im_recv, x_recv, send_sem, recv_sem, out_sem, passed,
 ):
     T = CHUNKS
     X = R // CORES
@@ -94,17 +95,32 @@
         pl.semaphore_signal(
             barrier, inc=1, device_id={"lat": lat, "rad": r}, device_id_type=MESH
         )
-    for j in range(1, M):
-        m, to_lat, to_rad = plane_peer(j)
+    pair = lat + 1 - 2 * lax.rem(lat, 2)
+    below, above = lat >= STEP, lat + STEP < L
+
+    def signal(sem, to_lat, to_rad):
         pl.semaphore_signal(
-            barrier, inc=1, device_id={"lat": to_lat, "rad": to_rad}, device_id_type=MESH
-        )
+            sem, inc=1, device_id={"lat": to_lat, "rad": to_rad}, device_id_type=MESH
+        )
+
+    def signal_below(sem):
+        pl.when(below)(lambda: signal(sem, lat - STEP, rad))
+
+    def signal_above(sem):
+        pl.when(above)(lambda: signal(sem, lat + STEP, rad))
+
+    for c in range(CORES):
+        signal(barrier, pair, chip * CORES + c)
+    signal_below(barrier)
+    signal_above(barrier)
     w_copy.start()
     for copy in inputs:
         copy.start()
     for q in range(T):
         own_copy(q).start()
-    pl.semaphore_wait(barrier, R - 1 + M - 1)
+    pl.semaphore_wait(
+        barrier, R - 1 + CORES + below.astype(jnp.int32) + above.astype(jnp.int32)
+    )
 
     AG, O1, I1, O2, I2, OT, IM, S1, S2, S3, OUT = range(11)
 
@@ -135,6 +151,10 @@
                 src.at[:, pl.ds(pl.multiple_of(to_core * half + q * CW, BLOCK), CW)],
                 slot(q, rad), AG, ag_recv.at[q], lat, to,
             )
+
+    up, down = passed.at[0], passed.at[1]
+    pl.when(jnp.logical_not(below))(lambda: signal_above(up))
+    pl.when(jnp.logical_not(above))(lambda: signal_below(down))
 
     w_copy.wait()
     for copy in inputs:
@@ -154,6 +174,17 @@
         return carry
 
     repeat(NB, prepare, 0)
+
+    @pl.when(below)
+    def _():
+        pl.semaphore_wait(up, 1)
+        signal_above(up)
+
+    @pl.when(above)
+    def _():
+        pl.semaphore_wait(down, 1)
+        signal_below(down)
+
     levels = to_ref.shape[0]
     eig_t[...] = jnp.transpose(jnp.broadcast_to(eig_ref[...], (levels, levels)))
 
@@ -389,37 +420,19 @@
         spread_at([(outer2, o_at + b), (inner2, i_at + b)], image[chip, b])
         return carry
 
-    def residual(b, value, carry):
-        final = modal[chip, b] - (coef[chip, 0] * image[chip, b] + coef[chip, 1] * value)
+    def second_pass(buf, at, first_block):
+        def step(i, carry):
+            b = first_block + i
+            twice[b] = operate(buf, at, chip, b, image[chip, b])
+            return carry
+
+        repeat(NB // 2, step, 0)
+
+    def residual(b, carry):
+        final = modal[chip, b] - (coef[chip, 0] * image[chip, b] + coef[chip, 1] * twice[b])
         return carry + final * final
 
-    def second_inside(i, carry):
-        b = inside + i
-        twice[b] = operate(inner2, i_at, chip, b, image[chip, b])
-        return carry
-
-    def residual_inside(i, carry):
-        b = inside + i
-        return residual(b, twice[b], carry)
-
-    outside = (NB // 2) * core
-
-    def second_outside(i, carry):
-        b = outside + i
-        return residual(b, operate(outer2, o_at, chip, b, image[chip, b]), carry)
-
-    repeat(NB, spread_own, 0)
-    inner_wait(inner2, 0, recv_sem.at[I2])
-    spread_halo(inner2, 0, inner_halo)
-    s2[chip] = plane_sum(s1, S1)
-    for j in range(1, X):
-        x = lax.rem(chip + j, X)
-        remote(s2.at[chip], s2.at[chip], S2, recv_sem.at[S2], lat, x * CORES + core)
-
-    repeat(NB // 2, second_inside, 0)
-
-    arrived(s2.at[pl.ds(0, X - 1)], recv_sem.at[S2])
-    for x in range(X):
+    def chebyshev(x):
         column = jnp.transpose(jnp.broadcast_to(s2[x], (BLOCK, BLOCK)))
         base, power = column[0:K], column[K:2 * K]
         upper = 1.5 * jnp.sqrt(power / (base + 1e-06))
@@ -433,13 +446,27 @@
         coef[x, 0] = (1.0 + rho_one * rho_zero) / center + second
         coef[x, 1] = -second / center
 
-    final = repeat(NB // 2, residual_inside, zero)
+    repeat(NB, spread_own, 0)
+    inner_wait(inner2, 0, recv_sem.at[I2])
+    spread_halo(inner2, 0, inner_halo)
+    second_pass(inner2, i_at, inside)
+    outer_wait(outer2, O2)
+    spread_halo(outer2, 0, outer_halo)
+    second_pass(outer2, o_at, (NB // 2) * core)
+
+    s2[chip] = plane_sum(s1, S1)
+    for j in range(1, X):
+        x = lax.rem(chip + j, X)
+        remote(s2.at[chip], s2.at[chip], S2, recv_sem.at[S2], lat, x * CORES + core)
+    chebyshev(chip)
+    s3[me] = lanes(repeat(NB, residual, zero))
+    plane_send(s3, S3)
+
+    arrived(s2.at[pl.ds(0, X - 1)], recv_sem.at[S2])
+    for j in range(1, X):
+        chebyshev(lax.rem(chip + j, X))
     for t in range(HC, T):
         finish(t)
-    outer_wait(outer2, O2)
-    spread_halo(outer2, 0, outer_halo)
-    s3[me] = lanes(repeat(NB // 2, second_outside, final))
-    plane_send(s3, S3)
     for t in range(HC):
         finish(t)
 
@@ -508,7 +535,7 @@
             pltpu.SMEM(neighbors.shape, jnp.int32),
             dma((5,)), dma(()), dma(()),
             dma((T,)), dma((T,)), dma((X - 1,)),
-            dma((11,)), dma((11,)), dma(()),
+            dma((11,)), dma((11,)), dma(()), pltpu.SemaphoreType.REGULAR((2,)),
         ],
         compiler_params=pltpu.CompilerParams(
             collective_id=0, has_side_effects=True, vmem_limit_bytes=67043328 - 4 * slab * nodes - 4096

time: 37.3 us -> 33.4 us (0.90)
  Pallas kernels: 35.2 us -> 31.3 us
    pallas_call x1, Pallas kernels: 35.2 us -> 31.3 us  [on_device(): pl.pallas_call(functools.partial(kernel, L, R, S), name='smoother', out_s...]
where the time goes in v2:
time: 33.4 us; the launch traced here: 33.3 us
  Pallas kernels  31.3 us (94%)
  local copies, waits for them, and re-layouts  1.31 us (4%)
  between operations  0.64 us (2%)
    pallas_call x1, Pallas kernels, on_device(): pl.pallas_call(functools.partial(kernel, L, R, S), name='smoother', out_s...  31.3 us
    unnamed x2, local copies, waits for them, and re-layouts  1.31 us

profile of v2, /device:TPU:0, one launch (start us, length us, event | category | flops | bytes accessed | tf_op | source)
XLA Modules:
  0.0 33.3 jit_solution(12666607698224852270)
XLA Ops:
  0.6 31.3 %smoother.1 = (f32[32,4096]{1,0:T(8,128)S(1)}, f32[1,32]{1,0:T(1,128)S(1)}) custom-call(f32[32,4096]{1,0:T(8,128)} %src.1, f32[31,4096]{1,0:T(8,128)} %w_hbm.1, f32[128,128]{1,0:T(8,128)} %to_hbm.1, f32[128,128]{1,0:T(8,128)} %from_hbm.1, f32[1,128]{1,0:T(1,128)} %bitcast.5, f32[32,128]{1,0:T(8,128)} %bitcast.4, s32[31,32]{1,0:T(8,128)} %nbr_hbm.1), custom_call_target="tpu_custom_call" | custom-call | tf_op jit(solution)/shard_map/smoother/pallas_call | solution.py:508
  32.0 0.8 %copy.11 = f32[32,4096]{1,0:T(8,128)} copy(f32[32,4096]{1,0:T(8,128)S(1)} %get-tuple-element.6) | data formatting | bytes 1048576
  32.8 0.5 %copy.12 = f32[32]{0:T(128)} copy(f32[32]{0:T(128)S(1)} %bitcast.3) | data formatting | bytes 256

commit v3 on v2

--- a/solution.py
+++ b/solution.py
@@ -10,9 +10,10 @@
 
 BLOCK = 128
 HALO = 8
-CHUNKS = 4
+CHUNKS = 8
+PARTS = 4
 GROUP = 8
-UNROLL = 4
+UNROLL = 8
 STEP = 2
 CORES = 2
 HIGHEST = lax.Precision.HIGHEST
@@ -23,8 +24,8 @@
     return jnp.dot(a, b, precision=HIGHEST, preferred_element_type=jnp.float32)
 
 
-def repeat(count, step, carry):
-    width = math.gcd(count, UNROLL)
+def repeat(count, step, carry, most=UNROLL):
+    width = math.gcd(count, most)
 
     def trip(n, carry):
         for j in range(width):
@@ -40,9 +41,9 @@
     L, R, S,
     src, w_hbm, to_hbm, from_hbm, eig_hbm, shift_hbm, nbr_hbm,
     out, res_ref,
-    gathered, wv, wr, outer1, inner1, outer2, inner2, others, modal, image, twice, eig_t, coef, part,
+    gathered, wv, wr, outer1, inner1, outer2, inner2, others, modal, image, twice, eig_t, coef, acc, part,
     rows, s1, s2, s3, to_ref, from_ref, eig_ref, nbr_ref,
-    in_sem, own_sem, w_sem, ag_recv, im_recv, x_recv, send_sem, recv_sem, out_sem, passed,
+    in_sem, own_sem, w_sem, ag_recv, x_recv, send_sem, recv_sem, out_sem, passed,
 ):
     T = CHUNKS
     X = R // CORES
@@ -90,13 +91,11 @@
         return m, lax.div(m, CORES), chip * CORES + lax.rem(m, CORES)
 
     barrier = pltpu.get_barrier_semaphore()
-    for j in range(1, R):
-        r = lax.rem(rad + j, R)
-        pl.semaphore_signal(
-            barrier, inc=1, device_id={"lat": lat, "rad": r}, device_id_type=MESH
-        )
-    pair = lat + 1 - 2 * lax.rem(lat, 2)
+    up, down, met, near_in, all_in = [passed.at[i] for i in range(5)]
+    gate = R - 1
+    is_gate = rad == gate
     below, above = lat >= STEP, lat + STEP < L
+    around = [(lat >= d, -d) for d in range(1, STEP + 1)] + [(lat + d < L, d) for d in range(1, STEP + 1)]
 
     def signal(sem, to_lat, to_rad):
         pl.semaphore_signal(
@@ -104,23 +103,30 @@
         )
 
     def signal_below(sem):
-        pl.when(below)(lambda: signal(sem, lat - STEP, rad))
+        pl.when(below)(lambda: signal(sem, lat - STEP, gate))
 
     def signal_above(sem):
-        pl.when(above)(lambda: signal(sem, lat + STEP, rad))
-
-    for c in range(CORES):
-        signal(barrier, pair, chip * CORES + c)
-    signal_below(barrier)
-    signal_above(barrier)
+        pl.when(above)(lambda: signal(sem, lat + STEP, gate))
+
+    for j in range(1, R):
+        r = lax.rem(rad + j, R)
+        pl.when(r != gate)(functools.partial(signal, barrier, lat, r))
     w_copy.start()
     for copy in inputs:
         copy.start()
     for q in range(T):
         own_copy(q).start()
-    pl.semaphore_wait(
-        barrier, R - 1 + CORES + below.astype(jnp.int32) + above.astype(jnp.int32)
-    )
+
+    @pl.when(jnp.logical_not(is_gate))
+    def _():
+        pl.semaphore_wait(barrier, R - 1)
+        pl.when(partner == gate)(lambda: signal(met, lat, gate))
+
+    @pl.when(is_gate)
+    def _():
+        pl.semaphore_wait(met, 1)
+        for there, d in around:
+            pl.when(there)(functools.partial(signal, barrier, lat + d, gate))
 
     AG, O1, I1, O2, I2, OT, IM, S1, S2, S3, OUT = range(11)
 
@@ -151,10 +157,6 @@
                 src.at[:, pl.ds(pl.multiple_of(to_core * half + q * CW, BLOCK), CW)],
                 slot(q, rad), AG, ag_recv.at[q], lat, to,
             )
-
-    up, down = passed.at[0], passed.at[1]
-    pl.when(jnp.logical_not(below))(lambda: signal_above(up))
-    pl.when(jnp.logical_not(above))(lambda: signal_below(down))
 
     w_copy.wait()
     for copy in inputs:
@@ -175,15 +177,26 @@
 
     repeat(NB, prepare, 0)
 
-    @pl.when(below)
+    @pl.when(is_gate)
     def _():
-        pl.semaphore_wait(up, 1)
-        signal_above(up)
-
-    @pl.when(above)
-    def _():
-        pl.semaphore_wait(down, 1)
-        signal_below(down)
+        pl.semaphore_wait(barrier, sum(there.astype(jnp.int32) for there, _ in around))
+        for r in range(R - 1):
+            signal(near_in, lat, r)
+        pl.when(jnp.logical_not(below))(lambda: signal_above(up))
+        pl.when(jnp.logical_not(above))(lambda: signal_below(down))
+
+        @pl.when(below)
+        def _():
+            pl.semaphore_wait(up, 1)
+            signal_above(up)
+
+        @pl.when(above)
+        def _():
+            pl.semaphore_wait(down, 1)
+            signal_below(down)
+
+        for r in range(R - 1):
+            signal(all_in, lat, r)
 
     levels = to_ref.shape[0]
     eig_t[...] = jnp.transpose(jnp.broadcast_to(eig_ref[...], (levels, levels)))
@@ -232,7 +245,7 @@
             spread_at([(buf, base + at + k)], buf[base + at + k])
             return carry
 
-        repeat(HALO, step, 0)
+        repeat(HALO, step, 0, UNROLL)
 
     def own_rows(x):
         return to_ref[pl.ds(pl.multiple_of(x * K, 8), K), :]
@@ -283,23 +296,34 @@
 
     zero = jnp.zeros((K, BLOCK), jnp.float32)
 
-    def first(t, buf, at, sums):
-        q = order(t, core)
+    def first(t, count, buf, at):
+        start = order(t, core) * (1 - core) + order(t + count - 1, core) * core
         step = first_pass(buf, at)
-        sums = repeat(CB, lambda i, carry: step(q * CB + i, carry), sums)
-        if t < HC:
-            outer_send(outer2, t, O2)
-            for j in range(1, X):
-                to = lax.rem(chip + j, X)
-                remote(
-                    image.at[chip, pl.ds(q * CB, CB)], image.at[chip, pl.ds(q * CB, CB)],
-                    IM, im_recv.at[q], lat, to * CORES + core,
-                )
-        if t >= T - HC:
-            inner_send(inner2, 0, t, I2, recv_sem.at[I2])
-        return sums
-
-    sums = (zero, zero)
+        sums = repeat(count * CB, lambda i, carry: step(start * CB + i, carry), (acc[0], acc[1]))
+        acc[0], acc[1] = sums
+        for t in range(t, t + count):
+            q = order(t, core)
+            if t < HC:
+                outer_send(outer2, t, O2)
+                for j in range(1, X):
+                    to = lax.rem(chip + j, X)
+                    remote(
+                        image.at[chip, pl.ds(q * CB, CB)], image.at[chip, pl.ds(q * CB, CB)],
+                        IM, recv_sem.at[IM], lat, to * CORES + core,
+                    )
+            if t >= T - HC:
+                inner_send(inner2, 0, t, I2, recv_sem.at[I2])
+
+    def outer_first(count):
+        outer_wait(outer1, O1)
+        spread_halo(outer1, 0, outer_halo)
+        first(0, count, outer1, o_at)
+
+    EARLY, GROUPED = max(HC, T - 3), T // PARTS
+    acc[0], acc[1] = zero, zero
+    late = jnp.logical_and(lat == 0, core == 0)
+    wraps = lat + 2 * core - 1 != other_lat
+    prompt = jnp.logical_not(late)
     for t in range(T):
         q = order(t, core)
         if t == 0:
@@ -313,6 +337,9 @@
             outer1[o_at + b] = value
             inner1[i_at + b] = value
             modal[chip, b] = value
+        if t == 0:
+            pl.when(jnp.logical_not(is_gate))(lambda: pl.semaphore_wait(near_in, 1))
+            pl.when(jnp.logical_and(jnp.logical_not(is_gate), wraps))(lambda: pl.semaphore_wait(all_in, 1))
         if t < HC:
             outer_send(outer1, t, O1)
         if t >= T - HC:
@@ -324,16 +351,27 @@
             )
         if t < T - 1:
             project_others(t)
-        if t == HC:
-            outer_wait(outer1, O1)
-            spread_halo(outer1, 0, outer_halo)
-        if t >= HC:
-            sums = first(t - HC, outer1, o_at, sums)
-    project_others(T - 1)
+        if t == EARLY:
+            pl.when(prompt)(functools.partial(outer_first, t - HC + 1))
+        if t > EARLY:
+            pl.when(prompt)(functools.partial(first, t - HC, 1, outer1, o_at))
+    pl.when(late)(functools.partial(outer_first, HC))
+    inside = (NB // 2) * (1 - core)
+    outside = (NB // 2) * core
+
+    def spread_own(at):
+        def step(i, carry):
+            b = at + i
+            spread_at([(outer2, o_at + b), (inner2, i_at + b)], image[chip, b])
+            return carry
+
+        repeat(NB // 2, step, 0, UNROLL)
+
+    spread_own(outside)
     inner_wait(inner1, 0, recv_sem.at[I1])
     spread_halo(inner1, 0, inner_halo)
-    for t in range(T - HC, T):
-        sums = first(t, inner1, i_at, sums)
+    for t in range(T - HC, T, GROUPED):
+        first(t, GROUPED, inner1, i_at)
 
     ones = jnp.ones((8, BLOCK), jnp.float32)
 
@@ -361,25 +399,9 @@
             total = total + buf[m]
         return total
 
-    s1[me] = lanes(jnp.concatenate(sums, axis=0))
+    s1[me] = lanes(jnp.concatenate([acc[0], acc[1]], axis=0))
+    pl.when(jnp.logical_not(jnp.logical_or(is_gate, wraps)))(lambda: pl.semaphore_wait(all_in, 1))
     plane_send(s1, S1)
-
-    inside = (NB // 2) * (1 - core)
-    for j in range(1, X):
-        x = lax.rem(chip + j, X)
-        base = (j - 1) * A * E
-        inner_wait(others, base, x_recv.at[j - 1])
-        spread_halo(others, base, inner_halo)
-    for j in range(1, X):
-        x = lax.rem(chip + j, X)
-        base = (j - 1) * A * E
-
-        def others_pass(i, carry, x=x, base=base):
-            b = inside + i
-            image[x, b] = operate(others, base + i_at, x, b, modal[x, b])
-            return carry
-
-        repeat(NB // 2, others_pass, 0)
 
     mine = jnp.concatenate(
         [
@@ -389,36 +411,27 @@
         axis=0,
     )
 
-    def columns(q):
-        return out.at[:, pl.ds(pl.multiple_of(core * half + q * CW, BLOCK), CW)]
+    FB = NB // PARTS
+
+    def columns(f):
+        return out.at[:, pl.ds(pl.multiple_of(core * half + f * FB * BLOCK, BLOCK), FB * BLOCK)]
 
     def columns_of(c):
         return out.at[:, pl.ds(c * half, half)]
 
-    def finish(t):
-        q = order(t, core)
-        if t < HC:
-            for j in range(1, X):
-                x = lax.rem(chip + j, X)
-                if j == 1:
-                    arrived(image.at[pl.ds(0, X - 1), pl.ds(q * CB, CB)], im_recv.at[q])
+    def finish(f):
         blocks = []
-        for i in range(CB):
-            b = q * CB + i
+        for b in range(f * FB, (f + 1) * FB):
             blocks.append(
                 jnp.concatenate(
                     [coef[x, 0] * modal[x, b] + coef[x, 1] * image[x, b] for x in range(X)], axis=0
                 )
             )
         product = dot(mine, jnp.concatenate(blocks, axis=1))
-        part[q, 0] = product[0:slab]
-        part[q, 1] = product[slab:K]
-        remote(part.at[q, 1], columns(q), OUT, recv_sem.at[OUT], lat, partner)
-        pltpu.make_async_copy(part.at[q, 0], columns(q), out_sem).start()
-
-    def spread_own(b, carry):
-        spread_at([(outer2, o_at + b), (inner2, i_at + b)], image[chip, b])
-        return carry
+        part[f, 0] = product[0:slab]
+        part[f, 1] = product[slab:K]
+        remote(part.at[f, 1], columns(f), OUT, recv_sem.at[OUT], lat, partner)
+        pltpu.make_async_copy(part.at[f, 0], columns(f), out_sem).start()
 
     def second_pass(buf, at, first_block):
         def step(i, carry):
@@ -446,14 +459,15 @@
         coef[x, 0] = (1.0 + rho_one * rho_zero) / center + second
         coef[x, 1] = -second / center
 
-    repeat(NB, spread_own, 0)
+    spread_own(inside)
     inner_wait(inner2, 0, recv_sem.at[I2])
     spread_halo(inner2, 0, inner_halo)
     second_pass(inner2, i_at, inside)
+    project_others(T - 1)
+
     outer_wait(outer2, O2)
     spread_halo(outer2, 0, outer_halo)
-    second_pass(outer2, o_at, (NB // 2) * core)
-
+    second_pass(outer2, o_at, outside)
     s2[chip] = plane_sum(s1, S1)
     for j in range(1, X):
         x = lax.rem(chip + j, X)
@@ -462,13 +476,28 @@
     s3[me] = lanes(repeat(NB, residual, zero))
     plane_send(s3, S3)
 
+    for j in range(1, X):
+        x = lax.rem(chip + j, X)
+        base = (j - 1) * A * E
+        inner_wait(others, base, x_recv.at[j - 1])
+        spread_halo(others, base, inner_halo)
+    for j in range(1, X):
+        x = lax.rem(chip + j, X)
+        base = (j - 1) * A * E
+
+        def others_pass(i, carry, x=x, base=base):
+            b = inside + i
+            image[x, b] = operate(others, base + i_at, x, b, modal[x, b])
+            return carry
+
+        repeat(NB // 2, others_pass, 0)
+
     arrived(s2.at[pl.ds(0, X - 1)], recv_sem.at[S2])
     for j in range(1, X):
         chebyshev(lax.rem(chip + j, X))
-    for t in range(HC, T):
-        finish(t)
-    for t in range(HC):
-        finish(t)
+    arrived(image.at[pl.ds(0, X - 1), pl.ds(0, HALO)], recv_sem.at[IM])
+    for f in range(PARTS):
+        finish(f)
 
     norm = jnp.sqrt(plane_sum(s3, S3) / (s2[chip] + 1e-06))
     res_ref[...] = jnp.where(core == 0, norm[:, 0:slab], norm[:, slab:2 * slab])
@@ -524,7 +553,8 @@
             pltpu.VMEM((NB, K, BLOCK), f32),
             pltpu.VMEM((levels, levels), f32),
             pltpu.VMEM((X, 2, K, BLOCK), f32),
-            pltpu.VMEM((T, 2, slab, CW), f32),
+            pltpu.VMEM((2, K, BLOCK), f32),
+            pltpu.VMEM((PARTS, 2, slab, half // PARTS), f32),
             pltpu.VMEM((NB, BLOCK), f32),
             pltpu.VMEM((M, 1, BLOCK), f32),
             pltpu.VMEM((X, 1, BLOCK), f32),
@@ -534,8 +564,8 @@
             pltpu.VMEM((1, levels), f32),
             pltpu.SMEM(neighbors.shape, jnp.int32),
             dma((5,)), dma(()), dma(()),
-            dma((T,)), dma((T,)), dma((X - 1,)),
-            dma((11,)), dma((11,)), dma(()), pltpu.SemaphoreType.REGULAR((2,)),
+            dma((T,)), dma((X - 1,)),
+            dma((11,)), dma((11,)), dma(()), pltpu.SemaphoreType.REGULAR((5,)),
         ],
         compiler_params=pltpu.CompilerParams(
             collective_id=0, has_side_effects=True, vmem_limit_bytes=67043328 - 4 * slab * nodes - 4096

time: 33.4 us -> 32.1 us (0.961)
  Pallas kernels: 31.3 us -> 30 us
    pallas_call x1, Pallas kernels: 31.3 us -> 30 us  [on_device(): pl.pallas_call(functools.partial(kernel, L, R, S), name='smoother', out_s...]
where the time goes in v3:
time: 32.1 us; the launch traced here: 32 us
  Pallas kernels  30 us (93%)
  local copies, waits for them, and re-layouts  1.31 us (4%)
  between operations  0.64 us (2%)
    pallas_call x1, Pallas kernels, on_device(): pl.pallas_call(functools.partial(kernel, L, R, S), name='smoother', out_s...  30 us
    unnamed x2, local copies, waits for them, and re-layouts  1.31 us

profile of v3, /device:TPU:0, one launch (start us, length us, event | category | flops | bytes accessed | tf_op | source)
XLA Modules:
  0.0 32.0 jit_solution(3099300113297360203)
XLA Ops:
  0.6 30.0 %smoother.1 = (f32[32,4096]{1,0:T(8,128)S(1)}, f32[1,32]{1,0:T(1,128)S(1)}) custom-call(f32[32,4096]{1,0:T(8,128)} %src.1, f32[31,4096]{1,0:T(8,128)} %w_hbm.1, f32[128,128]{1,0:T(8,128)} %to_hbm.1, f32[128,128]{1,0:T(8,128)} %from_hbm.1, f32[1,128]{1,0:T(1,128)} %bitcast.5, f32[32,128]{1,0:T(8,128)} %bitcast.4, s32[31,32]{1,0:T(8,128)} %nbr_hbm.1), custom_call_target="tpu_custom_call" | custom-call | tf_op jit(solution)/shard_map/smoother/pallas_call | solution.py:537
  30.7 0.8 %copy.11 = f32[32,4096]{1,0:T(8,128)} copy(f32[32,4096]{1,0:T(8,128)S(1)} %get-tuple-element.6) | data formatting | bytes 1048576
  31.5 0.5 %copy.12 = f32[32]{0:T(128)} copy(f32[32]{0:T(128)S(1)} %bitcast.3) | data formatting | bytes 256

commit v4 on v3

--- a/solution.py
+++ b/solution.py
@@ -12,6 +12,7 @@
 HALO = 8
 CHUNKS = 8
 PARTS = 4
+NEAR = 2
 GROUP = 8
 UNROLL = 8
 STEP = 2
@@ -41,8 +42,8 @@
     L, R, S,
     src, w_hbm, to_hbm, from_hbm, eig_hbm, shift_hbm, nbr_hbm,
     out, res_ref,
-    gathered, wv, wr, outer1, inner1, outer2, inner2, others, modal, image, twice, eig_t, coef, acc, part,
-    rows, s1, s2, s3, to_ref, from_ref, eig_ref, nbr_ref,
+    gathered, wv, wr, far_wv, far_wr, far, outer1, inner1, outer2, inner2, others, modal, image, twice, eig_t, coef, acc, part,
+    rows, far_rows, s1, s2, s3, to_ref, from_ref, eig_ref, nbr_ref, far_nbr,
     in_sem, own_sem, w_sem, ag_recv, x_recv, send_sem, recv_sem, out_sem, passed,
 ):
     T = CHUNKS
@@ -56,6 +57,8 @@
     HC = HALO // CB
     CW = CB * BLOCK
     E = NB + HALO
+    F = NEAR + 2 * HALO
+    NC = NEAR // CB
     A = -(-S // GROUP)
     lat = lax.axis_index("lat")
     rad = lax.axis_index("rad")
@@ -64,6 +67,7 @@
     partner = chip * CORES + (1 - core)
     me = lat * CORES + core
     other_lat = lax.rem(lat + (L - 1) * (1 - core) + core, L)
+    wraps = lat + 2 * core - 1 != other_lat
 
     def order(t, c):
         return t * (1 - c) + (T - 1 - t) * c
@@ -128,7 +132,7 @@
         for there, d in around:
             pl.when(there)(functools.partial(signal, barrier, lat + d, gate))
 
-    AG, O1, I1, O2, I2, OT, IM, S1, S2, S3, OUT = range(11)
+    AG, O1, I1, O2, I2, OT, IM, S1, S2, S3, OUT, FAR, FAR_W, FAR_ROWS, FAR_NBR = range(15)
 
     def remote(src_ref, dst_ref, kind, recv, lat_to, rad_to):
         pltpu.make_async_remote_copy(
@@ -163,17 +167,42 @@
         copy.wait()
     row_id = lax.broadcasted_iota(jnp.int32, (A * GROUP, BLOCK), 0)
 
-    def prepare(b, carry):
-        wr[b, pl.ds((A - 1) * GROUP, GROUP), :] = jnp.zeros((GROUP, BLOCK), jnp.float32)
-        wr[b, pl.ds(0, S), :] = wv[:, pl.ds(pl.multiple_of(b * BLOCK, BLOCK), BLOCK)]
-        tile = wr[b, pl.ds(0, A * GROUP), :]
+    def prepare_from(raw, shift, row_at, ready, b):
+        ready[b, pl.ds((A - 1) * GROUP, GROUP), :] = jnp.zeros((GROUP, BLOCK), jnp.float32)
+        ready[b, pl.ds(0, S), :] = raw[:, pl.ds(pl.multiple_of(b * BLOCK, BLOCK), BLOCK)]
+        tile = ready[b, pl.ds(0, A * GROUP), :]
         placed = tile
         for c in range(1, GROUP):
             placed = jnp.where(lax.rem(row_id, GROUP) == c, pltpu.roll(tile, c, 1), placed)
-        wr[b, pl.ds(0, A * GROUP), :] = placed
-        diagonal = jnp.sum(tile, axis=0, keepdims=True) + rows[pl.ds(b, 1), :]
-        wr[b, pl.ds(A * GROUP, GROUP), :] = jnp.broadcast_to(diagonal, (GROUP, BLOCK))
+        ready[b, pl.ds(0, A * GROUP), :] = placed
+        diagonal = jnp.sum(tile, axis=0, keepdims=True) + shift[pl.ds(row_at + b, 1), :]
+        ready[b, pl.ds(A * GROUP, GROUP), :] = jnp.broadcast_to(diagonal, (GROUP, BLOCK))
+
+    def prepare(b, carry):
+        prepare_from(wv, rows, 0, wr, b)
         return carry
+
+    row_tile = far_rows.shape[0]
+
+    def prepare_far(b, carry):
+        prepare_from(far_wv, far_rows, (row_tile - NEAR) * (1 - core), far_wr, b)
+        return carry
+
+    far_inputs = ((far_wv, FAR_W), (far_rows, FAR_ROWS), (far_nbr, FAR_NBR))
+
+    def far_start():
+        parts = (
+            w_hbm.at[:, pl.ds(pl.multiple_of(core * (nodes - NEAR * BLOCK), BLOCK), NEAR * BLOCK)],
+            shift_hbm.at[pl.ds(pl.multiple_of(core * (nodes // BLOCK - row_tile), 8), row_tile), :],
+            nbr_hbm,
+        )
+        for part_ref, (ref, kind) in zip(parts, far_inputs):
+            remote(part_ref, ref, kind, recv_sem.at[kind], other_lat, partner)
+
+    def far_ready():
+        for ref, kind in far_inputs:
+            arrived(ref, recv_sem.at[kind])
+        repeat(NEAR, prepare_far, 0)
 
     repeat(NB, prepare, 0)
 
@@ -182,6 +211,7 @@
         pl.semaphore_wait(barrier, sum(there.astype(jnp.int32) for there, _ in around))
         for r in range(R - 1):
             signal(near_in, lat, r)
+        pl.when(jnp.logical_not(wraps))(far_start)
         pl.when(jnp.logical_not(below))(lambda: signal_above(up))
         pl.when(jnp.logical_not(above))(lambda: signal_below(down))
 
@@ -197,6 +227,11 @@
 
         for r in range(R - 1):
             signal(all_in, lat, r)
+
+    @pl.when(jnp.logical_not(is_gate))
+    def _():
+        pl.semaphore_wait(near_in, 1)
+        pl.when(jnp.logical_not(wraps))(far_start)
 
     levels = to_ref.shape[0]
     eig_t[...] = jnp.transpose(jnp.broadcast_to(eig_ref[...], (levels, levels)))
@@ -220,8 +255,8 @@
             kind, recv_sem.at[kind], other_lat, partner,
         )
 
-    def outer_wait(buf, kind):
-        arrived(buf.at[pl.ds(outer_halo, HALO)], recv_sem.at[kind])
+    def outer_wait(buf, skip, kind):
+        arrived(buf.at[pl.ds(outer_halo + core * skip, HALO - skip)], recv_sem.at[kind])
 
     def inner_send(buf, base, t, kind, recv):
         q = order(t, core)
@@ -237,15 +272,57 @@
     def spread_at(targets, value):
         for a in range(1, A):
             moved = pltpu.roll(value, BLOCK - a * GROUP, 1)
-            for buf, k in targets:
-                buf[a * E + k] = moved
-
-    def spread_halo(buf, base, at):
+            for buf, stride, k in targets:
+                buf[a * stride + k] = moved
+
+    def spread_halo(buf, base, at, count=HALO):
         def step(k, carry):
-            spread_at([(buf, base + at + k)], buf[base + at + k])
+            spread_at([(buf, E, base + at + k)], buf[base + at + k])
             return carry
 
-        repeat(HALO, step, 0, UNROLL)
+        repeat(count, step, 0)
+
+    far_own = (NEAR + HALO) * (1 - core) - (NB - HALO) * core
+    far_halo = NEAR * (1 - core) + HALO * core
+    far_more = 2 * HALO * core
+
+    def far_at(b):
+        return b + HALO * (1 - core) - (NB - NEAR - HALO) * core
+
+    def far_send(t):
+        q = order(t, core)
+        remote(
+            outer1.at[pl.ds(o_at + q * CB, CB)], far.at[pl.ds(far_at(q * CB), CB)],
+            FAR, recv_sem.at[FAR], other_lat, partner,
+        )
+
+    def spread_outer_halo():
+        def step(k, carry):
+            value = outer1[outer_halo + k]
+            far[far_halo + k] = value
+            spread_at([(outer1, E, outer_halo + k), (far, F, far_halo + k)], value)
+            return carry
+
+        repeat(HALO, step, 0)
+
+    def far_pass():
+        arrived(far.at[pl.ds(far_more, NEAR)], recv_sem.at[FAR])
+
+        def spread_more(k, carry):
+            spread_at([(far, F, far_more + k)], far[far_more + k])
+            return carry
+
+        def step(i, carry):
+            at = HALO + i
+            column = (nodes // BLOCK - NEAR) * (1 - core) + i
+            value = operate(far, F, at, far_wr, i, far_nbr, column, chip, far[at])
+            k = outer_halo + (HALO - NEAR) * (1 - core) + i
+            outer2[k] = value
+            spread_at([(outer2, E, k)], value)
+            return carry
+
+        repeat(NEAR, spread_more, 0)
+        repeat(NEAR, step, 0)
 
     def own_rows(x):
         return to_ref[pl.ds(pl.multiple_of(x * K, 8), K), :]
@@ -264,29 +341,32 @@
                 inner_send(others, base, t, OT, x_recv.at[j - 1])
             for i in range(CB):
                 spread_at(
-                    [(others, base + i_at + q * CB + i)], product[:, i * BLOCK:(i + 1) * BLOCK]
+                    [(others, E, base + i_at + q * CB + i)], product[:, i * BLOCK:(i + 1) * BLOCK]
                 )
 
-    def operate(buf, base, x, b, field):
+    def operate(buf, stride, at, weight, b, table, column, x, field):
         total = None
         for c in range(GROUP):
             inner = None
             for a in range(A):
                 s = a * GROUP + c
                 if s < S:
-                    n = nbr_ref[s, core * NB + b]
-                    term = buf[base + a * E + b + n] * wr[b, pl.ds(s, 1), :]
+                    n = table[s, column]
+                    term = buf[a * stride + at + n] * weight[b, pl.ds(s, 1), :]
                     inner = term if inner is None else inner + term
             if inner is not None:
                 moved = inner if c == 0 else pltpu.roll(inner, BLOCK - c, 1)
                 total = moved if total is None else total + moved
         eig = eig_t[pl.ds(pl.multiple_of(x * K, 8), K), :]
-        return (wr[b, pl.ds(A * GROUP, 1), :] + eig) * field - total
+        return (weight[b, pl.ds(A * GROUP, 1), :] + eig) * field - total
+
+    def operate_own(buf, base, x, b, field):
+        return operate(buf, E, base + b, wr, b, nbr_ref, core * NB + b, x, field)
 
     def first_pass(buf, at):
         def step(b, carry):
             field = modal[chip, b]
-            value = operate(buf, at, chip, b, field)
+            value = operate_own(buf, at, chip, b, field)
             outer2[o_at + b] = value
             inner2[i_at + b] = value
             image[chip, b] = value
@@ -295,6 +375,15 @@
         return step
 
     zero = jnp.zeros((K, BLOCK), jnp.float32)
+
+    def image_send(t):
+        q = order(t, core)
+        for j in range(1, X):
+            to = lax.rem(chip + j, X)
+            remote(
+                image.at[chip, pl.ds(q * CB, CB)], image.at[chip, pl.ds(q * CB, CB)],
+                IM, recv_sem.at[IM], lat, to * CORES + core,
+            )
 
     def first(t, count, buf, at):
         start = order(t, core) * (1 - core) + order(t + count - 1, core) * core
@@ -303,26 +392,21 @@
         acc[0], acc[1] = sums
         for t in range(t, t + count):
             q = order(t, core)
-            if t < HC:
+            if NC <= t < HC:
                 outer_send(outer2, t, O2)
-                for j in range(1, X):
-                    to = lax.rem(chip + j, X)
-                    remote(
-                        image.at[chip, pl.ds(q * CB, CB)], image.at[chip, pl.ds(q * CB, CB)],
-                        IM, recv_sem.at[IM], lat, to * CORES + core,
-                    )
+            if t < HC // 2:
+                image_send(t)
             if t >= T - HC:
                 inner_send(inner2, 0, t, I2, recv_sem.at[I2])
 
     def outer_first(count):
-        outer_wait(outer1, O1)
-        spread_halo(outer1, 0, outer_halo)
+        outer_wait(outer1, 0, O1)
+        spread_outer_halo()
         first(0, count, outer1, o_at)
 
-    EARLY, GROUPED = max(HC, T - 3), T // PARTS
+    EARLY, GROUPED, READY = max(HC, T - 3), T // PARTS, HC - 1
     acc[0], acc[1] = zero, zero
     late = jnp.logical_and(lat == 0, core == 0)
-    wraps = lat + 2 * core - 1 != other_lat
     prompt = jnp.logical_not(late)
     for t in range(T):
         q = order(t, core)
@@ -337,24 +421,41 @@
             outer1[o_at + b] = value
             inner1[i_at + b] = value
             modal[chip, b] = value
+            if t < HC:
+                far[far_own + b] = value
         if t == 0:
-            pl.when(jnp.logical_not(is_gate))(lambda: pl.semaphore_wait(near_in, 1))
             pl.when(jnp.logical_and(jnp.logical_not(is_gate), wraps))(lambda: pl.semaphore_wait(all_in, 1))
         if t < HC:
             outer_send(outer1, t, O1)
+        elif t < HC + NC:
+            pl.when(prompt)(functools.partial(far_send, t))
         if t >= T - HC:
             inner_send(inner1, 0, t, I1, recv_sem.at[I1])
         for i in range(CB):
             b = q * CB + i
             spread_at(
-                [(outer1, o_at + b), (inner1, i_at + b)], product[:, i * BLOCK:(i + 1) * BLOCK]
+                [(outer1, E, o_at + b), (inner1, E, i_at + b)]
+                + ([(far, F, far_own + b)] if t < HC else []),
+                product[:, i * BLOCK:(i + 1) * BLOCK],
             )
         if t < T - 1:
             project_others(t)
+        if t == READY:
+            pl.when(jnp.logical_not(wraps))(far_ready)
+        if t == HC + NC - 1:
+            pl.when(jnp.logical_and(prompt, wraps))(far_start)
         if t == EARLY:
+
+            @pl.when(late)
+            def _():
+                for n in range(HC, HC + NC):
+                    far_send(n)
+                far_start()
+
             pl.when(prompt)(functools.partial(outer_first, t - HC + 1))
         if t > EARLY:
             pl.when(prompt)(functools.partial(first, t - HC, 1, outer1, o_at))
+
     pl.when(late)(functools.partial(outer_first, HC))
     inside = (NB // 2) * (1 - core)
     outside = (NB // 2) * core
@@ -362,7 +463,7 @@
     def spread_own(at):
         def step(i, carry):
             b = at + i
-            spread_at([(outer2, o_at + b), (inner2, i_at + b)], image[chip, b])
+            spread_at([(outer2, E, o_at + b), (inner2, E, i_at + b)], image[chip, b])
             return carry
 
         repeat(NB // 2, step, 0, UNROLL)
@@ -387,21 +488,35 @@
             )
         return line[0:1]
 
-    def plane_send(buf, kind):
+    def plane_send(ref, kind):
         for j in range(1, M):
             m, to_lat, to_rad = plane_peer(j)
-            remote(buf.at[me], buf.at[me], kind, recv_sem.at[kind], to_lat, to_rad)
-
-    def plane_sum(buf, kind):
-        arrived(buf.at[pl.ds(0, M - 1)], recv_sem.at[kind])
+            remote(ref, ref, kind, recv_sem.at[kind], to_lat, to_rad)
+
+    def plane_sum(buf):
         total = buf[0]
         for m in range(1, M):
             total = total + buf[m]
         return total
 
-    s1[me] = lanes(jnp.concatenate([acc[0], acc[1]], axis=0))
+    def cross_send():
+        def step(n, carry):
+            to = lax.rem(chip + 1 + lax.div(n, M), X)
+            m = lax.rem(me + lax.rem(n, M), M)
+            remote(
+                s1.at[chip, me], s1.at[chip, me], S2, recv_sem.at[S2],
+                lax.div(m, CORES), to * CORES + lax.rem(m, CORES),
+            )
+            return carry
+
+        lax.fori_loop(0, (X - 1) * M, step, 0)
+
+    s1[chip, me] = lanes(jnp.concatenate([acc[0], acc[1]], axis=0))
     pl.when(jnp.logical_not(jnp.logical_or(is_gate, wraps)))(lambda: pl.semaphore_wait(all_in, 1))
-    plane_send(s1, S1)
+    plane_send(s1.at[chip, me], S1)
+    cross_send()
+    for t in range(HC // 2, HC):
+        image_send(t)
 
     mine = jnp.concatenate(
         [
@@ -436,7 +551,7 @@
     def second_pass(buf, at, first_block):
         def step(i, carry):
             b = first_block + i
-            twice[b] = operate(buf, at, chip, b, image[chip, b])
+            twice[b] = operate_own(buf, at, chip, b, image[chip, b])
             return carry
 
         repeat(NB // 2, step, 0)
@@ -446,6 +561,7 @@
         return carry + final * final
 
     def chebyshev(x):
+        s2[x] = plane_sum(s1.at[x])
         column = jnp.transpose(jnp.broadcast_to(s2[x], (BLOCK, BLOCK)))
         base, power = column[0:K], column[K:2 * K]
         upper = 1.5 * jnp.sqrt(power / (base + 1e-06))
@@ -465,16 +581,15 @@
     second_pass(inner2, i_at, inside)
     project_others(T - 1)
 
-    outer_wait(outer2, O2)
-    spread_halo(outer2, 0, outer_halo)
+    pl.when(wraps)(far_ready)
+    far_pass()
+    outer_wait(outer2, NEAR, O2)
+    spread_halo(outer2, 0, outer_halo + core * NEAR, HALO - NEAR)
     second_pass(outer2, o_at, outside)
-    s2[chip] = plane_sum(s1, S1)
-    for j in range(1, X):
-        x = lax.rem(chip + j, X)
-        remote(s2.at[chip], s2.at[chip], S2, recv_sem.at[S2], lat, x * CORES + core)
+    arrived(s1.at[0, pl.ds(0, M - 1)], recv_sem.at[S1])
     chebyshev(chip)
     s3[me] = lanes(repeat(NB, residual, zero))
-    plane_send(s3, S3)
+    plane_send(s3.at[me], S3)
 
     for j in range(1, X):
         x = lax.rem(chip + j, X)
@@ -487,32 +602,37 @@
 
         def others_pass(i, carry, x=x, base=base):
             b = inside + i
-            image[x, b] = operate(others, base + i_at, x, b, modal[x, b])
+            image[x, b] = operate_own(others, base + i_at, x, b, modal[x, b])
             return carry
 
         repeat(NB // 2, others_pass, 0)
 
-    arrived(s2.at[pl.ds(0, X - 1)], recv_sem.at[S2])
+    arrived(s1.at[pl.ds(0, X - 1)], recv_sem.at[S2])
     for j in range(1, X):
         chebyshev(lax.rem(chip + j, X))
     arrived(image.at[pl.ds(0, X - 1), pl.ds(0, HALO)], recv_sem.at[IM])
     for f in range(PARTS):
         finish(f)
 
-    norm = jnp.sqrt(plane_sum(s3, S3) / (s2[chip] + 1e-06))
+    arrived(s3.at[pl.ds(0, M - 1)], recv_sem.at[S3])
+    norm = jnp.sqrt(plane_sum(s3) / (s2[chip] + 1e-06))
     res_ref[...] = jnp.where(core == 0, norm[:, 0:slab], norm[:, slab:2 * slab])
 
     everything = columns_of(0)
     pltpu.make_async_copy(everything, everything, out_sem).wait()
     whole(columns_of(0), OUT, recv_sem.at[OUT]).wait()
     whole(gathered.at[:, pl.ds(0, (R - 1) * slab), :], AG, ag_recv.at[0]).wait_send()
-    for kind in (O1, I1, O2, I2):
+    for kind in (O1, I1, I2):
         whole(outer1.at[pl.ds(0, HALO)], kind, recv_sem.at[kind]).wait_send()
+    whole(outer1.at[pl.ds(0, HALO - NEAR)], O2, recv_sem.at[O2]).wait_send()
+    whole(outer1.at[pl.ds(0, NEAR)], FAR, recv_sem.at[FAR]).wait_send()
+    for ref, kind in far_inputs:
+        whole(ref, kind, recv_sem.at[kind]).wait_send()
     whole(others.at[pl.ds(0, (X - 1) * HALO)], OT, recv_sem.at[OT]).wait_send()
     whole(image.at[pl.ds(0, X - 1), pl.ds(0, HALO)], IM, recv_sem.at[IM]).wait_send()
-    for buf, kind in ((s1, S1), (s3, S3)):
-        whole(buf.at[pl.ds(0, M - 1)], kind, recv_sem.at[kind]).wait_send()
-    whole(s2.at[pl.ds(0, X - 1)], S2, recv_sem.at[S2]).wait_send()
+    for kind in (S1, S3):
+        whole(s3.at[pl.ds(0, M - 1)], kind, recv_sem.at[kind]).wait_send()
+    whole(s1.at[pl.ds(0, X - 1)], S2, recv_sem.at[S2]).wait_send()
 
 
 def on_device(L, R, source, to_modes, from_modes, eigenvalue, shifts, weights, neighbors):
@@ -547,6 +667,9 @@
             pltpu.VMEM((T, levels, CW), f32),
             pltpu.VMEM((S, half), f32),
             pltpu.VMEM((NB, (A + 1) * GROUP, BLOCK), f32),
+            pltpu.VMEM((S, NEAR * BLOCK), f32),
+            pltpu.VMEM((NEAR, (A + 1) * GROUP, BLOCK), f32),
+            pltpu.VMEM((A * (NEAR + 2 * HALO), K, BLOCK), f32),
             window(1), window(1), window(1), window(1), window(X - 1),
             pltpu.VMEM((X, NB, K, BLOCK), f32),
             pltpu.VMEM((X, NB, K, BLOCK), f32),
@@ -556,16 +679,18 @@
             pltpu.VMEM((2, K, BLOCK), f32),
             pltpu.VMEM((PARTS, 2, slab, half // PARTS), f32),
             pltpu.VMEM((NB, BLOCK), f32),
-            pltpu.VMEM((M, 1, BLOCK), f32),
+            pltpu.VMEM((GROUP, BLOCK), f32),
+            pltpu.VMEM((X, M, 1, BLOCK), f32),
             pltpu.VMEM((X, 1, BLOCK), f32),
             pltpu.VMEM((M, 1, BLOCK), f32),
             pltpu.VMEM((levels, levels), f32),
             pltpu.VMEM((levels, levels), f32),
             pltpu.VMEM((1, levels), f32),
             pltpu.SMEM(neighbors.shape, jnp.int32),
+            pltpu.SMEM(neighbors.shape, jnp.int32),
             dma((5,)), dma(()), dma(()),
             dma((T,)), dma((X - 1,)),
-            dma((11,)), dma((11,)), dma(()), pltpu.SemaphoreType.REGULAR((5,)),
+            dma((15,)), dma((15,)), dma(()), pltpu.SemaphoreType.REGULAR((5,)),
         ],
         compiler_params=pltpu.CompilerParams(
             collective_id=0, has_side_effects=True, vmem_limit_bytes=67043328 - 4 * slab * nodes - 4096

time: 32.1 us -> 31.9 us (level)
  no operation moved by 1% of the time
where the time goes in v4:
time: 31.9 us; the launch traced here: 31.7 us
  Pallas kernels  29.8 us (93%)
  local copies, waits for them, and re-layouts  1.31 us (4%)
  between operations  0.64 us (2%)
    pallas_call x1, Pallas kernels, on_device(): pl.pallas_call(functools.partial(kernel, L, R, S), name='smoother', out_s...  29.8 us
    unnamed x2, local copies, waits for them, and re-layouts  1.31 us

profile of v4, /device:TPU:0, one launch (start us, length us, event | category | flops | bytes accessed | tf_op | source)
XLA Modules:
  0.0 31.7 jit_solution(1574282806373160627)
XLA Ops:
  0.6 29.8 %smoother.1 = (f32[32,4096]{1,0:T(8,128)S(1)}, f32[1,32]{1,0:T(1,128)S(1)}) custom-call(f32[32,4096]{1,0:T(8,128)} %src.1, f32[31,4096]{1,0:T(8,128)} %w_hbm.1, f32[128,128]{1,0:T(8,128)} %to_hbm.1, f32[128,128]{1,0:T(8,128)} %from_hbm.1, f32[1,128]{1,0:T(1,128)} %bitcast.5, f32[32,128]{1,0:T(8,128)} %bitcast.4, s32[31,32]{1,0:T(8,128)} %nbr_hbm.1), custom_call_target="tpu_custom_call" | custom-call | tf_op jit(solution)/shard_map/smoother/pallas_call | solution.py:657
  30.4 0.8 %copy.11 = f32[32,4096]{1,0:T(8,128)} copy(f32[32,4096]{1,0:T(8,128)S(1)} %get-tuple-element.6) | data formatting | bytes 1048576
  31.2 0.5 %copy.12 = f32[32]{0:T(128)} copy(f32[32]{0:T(128)S(1)} %bitcast.3) | data formatting | bytes 256

commit v5 on v4

--- a/solution.py
+++ b/solution.py
@@ -1,5 +1,4 @@
 import functools
-import math
 
 import jax
 import jax.numpy as jnp
@@ -21,12 +20,22 @@
 MESH = pl.DeviceIdType.MESH
 
 
+def halves(v):
+    high = v.astype(jnp.bfloat16)
+    return high, (v - high.astype(jnp.float32)).astype(jnp.bfloat16)
+
+
 def dot(a, b):
-    return jnp.dot(a, b, precision=HIGHEST, preferred_element_type=jnp.float32)
+    (a_high, a_low), (b_high, b_low) = halves(a), halves(b)
+    left = jnp.concatenate([a_high, a_high], axis=1)
+    right = jnp.concatenate([b_high, b_low], axis=0)
+    return jnp.dot(left, right, preferred_element_type=jnp.float32) + jnp.dot(
+        a_low, b_high, preferred_element_type=jnp.float32
+    )
 
 
 def repeat(count, step, carry, most=UNROLL):
-    width = math.gcd(count, most)
+    width = max(n for n in range(1, min(count, most) + 1) if count % n == 0)
 
     def trip(n, carry):
         for j in range(width):
@@ -402,8 +411,12 @@
     def outer_first(count):
         outer_wait(outer1, 0, O1)
         spread_outer_halo()
-        first(0, count, outer1, o_at)
-
+        for t in range(NC, count):
+            first(t, 1, outer1, o_at)
+        if count == HC:
+            first(0, NC, outer1, o_at)
+
+    LAST = 2
     EARLY, GROUPED, READY = max(HC, T - 3), T // PARTS, HC - 1
     acc[0], acc[1] = zero, zero
     late = jnp.logical_and(lat == 0, core == 0)
@@ -438,7 +451,7 @@
                 + ([(far, F, far_own + b)] if t < HC else []),
                 product[:, i * BLOCK:(i + 1) * BLOCK],
             )
-        if t < T - 1:
+        if t < T - LAST:
             project_others(t)
         if t == READY:
             pl.when(jnp.logical_not(wraps))(far_ready)
@@ -455,6 +468,8 @@
             pl.when(prompt)(functools.partial(outer_first, t - HC + 1))
         if t > EARLY:
             pl.when(prompt)(functools.partial(first, t - HC, 1, outer1, o_at))
+        if t == T - 1:
+            pl.when(prompt)(functools.partial(first, 0, NC, outer1, o_at))
 
     pl.when(late)(functools.partial(outer_first, HC))
     inside = (NB // 2) * (1 - core)
@@ -474,11 +489,11 @@
     for t in range(T - HC, T, GROUPED):
         first(t, GROUPED, inner1, i_at)
 
-    ones = jnp.ones((8, BLOCK), jnp.float32)
+    ones = jnp.ones((8, 2 * BLOCK), jnp.bfloat16)
 
     def lanes(values):
         line = lax.dot_general(
-            ones, values, (((1,), (1,)), ((), ())), precision=HIGHEST,
+            ones, jnp.concatenate(halves(values), axis=1), (((1,), (1,)), ((), ())),
             preferred_element_type=jnp.float32,
         )
         width = line.shape[1]
@@ -536,7 +551,8 @@
 
     def finish(f):
         blocks = []
-        for b in range(f * FB, (f + 1) * FB):
+        for i in range(FB):
+            b = f * FB + i
             blocks.append(
                 jnp.concatenate(
                     [coef[x, 0] * modal[x, b] + coef[x, 1] * image[x, b] for x in range(X)], axis=0
@@ -579,10 +595,28 @@
     inner_wait(inner2, 0, recv_sem.at[I2])
     spread_halo(inner2, 0, inner_halo)
     second_pass(inner2, i_at, inside)
-    project_others(T - 1)
+    def others_image():
+        for t in range(T - LAST, T):
+            project_others(t)
+        for j in range(1, X):
+            x = lax.rem(chip + j, X)
+            base = (j - 1) * A * E
+            inner_wait(others, base, x_recv.at[j - 1])
+            spread_halo(others, base, inner_halo)
+        for j in range(1, X):
+            x = lax.rem(chip + j, X)
+            base = (j - 1) * A * E
+
+            def others_pass(i, carry, x=x, base=base):
+                b = inside + i
+                image[x, b] = operate_own(others, base + i_at, x, b, modal[x, b])
+                return carry
+
+            repeat(NB // 2, others_pass, 0)
 
     pl.when(wraps)(far_ready)
     far_pass()
+    pl.when(lat == 0)(others_image)
     outer_wait(outer2, NEAR, O2)
     spread_halo(outer2, 0, outer_halo + core * NEAR, HALO - NEAR)
     second_pass(outer2, o_at, outside)
@@ -591,28 +625,15 @@
     s3[me] = lanes(repeat(NB, residual, zero))
     plane_send(s3.at[me], S3)
 
-    for j in range(1, X):
-        x = lax.rem(chip + j, X)
-        base = (j - 1) * A * E
-        inner_wait(others, base, x_recv.at[j - 1])
-        spread_halo(others, base, inner_halo)
-    for j in range(1, X):
-        x = lax.rem(chip + j, X)
-        base = (j - 1) * A * E
-
-        def others_pass(i, carry, x=x, base=base):
-            b = inside + i
-            image[x, b] = operate_own(others, base + i_at, x, b, modal[x, b])
-            return carry
-
-        repeat(NB // 2, others_pass, 0)
-
     arrived(s1.at[pl.ds(0, X - 1)], recv_sem.at[S2])
     for j in range(1, X):
         chebyshev(lax.rem(chip + j, X))
     arrived(image.at[pl.ds(0, X - 1), pl.ds(0, HALO)], recv_sem.at[IM])
-    for f in range(PARTS):
-        finish(f)
+    for f in range(PARTS // 2):
+        finish(f + (PARTS // 2) * core)
+    pl.when(lat != 0)(others_image)
+    for f in range(PARTS // 2):
+        finish(f + (PARTS // 2) * (1 - core))
 
     arrived(s3.at[pl.ds(0, M - 1)], recv_sem.at[S3])
     norm = jnp.sqrt(plane_sum(s3) / (s2[chip] + 1e-06))

time: 31.9 us -> 31 us (0.972)
  Pallas kernels: 29.8 us -> 28.9 us
    pallas_call x1, Pallas kernels: 29.8 us -> 28.9 us  [on_device(): pl.pallas_call(functools.partial(kernel, L, R, S), name='smoother', out_s...]
where the time goes in v5:
time: 31 us; the launch traced here: 30.9 us
  Pallas kernels  28.9 us (93%)
  local copies, waits for them, and re-layouts  1.31 us (4%)
  between operations  0.64 us (2%)
    pallas_call x1, Pallas kernels, on_device(): pl.pallas_call(functools.partial(kernel, L, R, S), name='smoother', out_s...  28.9 us
    unnamed x2, local copies, waits for them, and re-layouts  1.31 us

profile of v5, /device:TPU:0, one launch (start us, length us, event | category | flops | bytes accessed | tf_op | source)
XLA Modules:
  0.0 30.9 jit_solution(2195704907861007457)
XLA Ops:
  0.6 28.9 %smoother.1 = (f32[32,4096]{1,0:T(8,128)S(1)}, f32[1,32]{1,0:T(1,128)S(1)}) custom-call(f32[32,4096]{1,0:T(8,128)} %src.1, f32[31,4096]{1,0:T(8,128)} %w_hbm.1, f32[128,128]{1,0:T(8,128)} %to_hbm.1, f32[128,128]{1,0:T(8,128)} %from_hbm.1, f32[1,128]{1,0:T(1,128)} %bitcast.5, f32[32,128]{1,0:T(8,128)} %bitcast.4, s32[31,32]{1,0:T(8,128)} %nbr_hbm.1), custom_call_target="tpu_custom_call" | custom-call | tf_op jit(solution)/shard_map/smoother/pallas_call | solution.py:678
  29.6 0.8 %copy.11 = f32[32,4096]{1,0:T(8,128)} copy(f32[32,4096]{1,0:T(8,128)S(1)} %get-tuple-element.6) | data formatting | bytes 1048576
  30.4 0.5 %copy.12 = f32[32]{0:T(128)} copy(f32[32]{0:T(128)S(1)} %bitcast.3) | data formatting | bytes 256

commit v6 on v5

--- a/solution.py
+++ b/solution.py
@@ -416,8 +416,7 @@
         if count == HC:
             first(0, NC, outer1, o_at)
 
-    LAST = 2
-    EARLY, GROUPED, READY = max(HC, T - 3), T // PARTS, HC - 1
+    LAST, EARLY, GROUPED, READY = T // 4, T * 11 // 16, T // PARTS, HC - 1
     acc[0], acc[1] = zero, zero
     late = jnp.logical_and(lat == 0, core == 0)
     prompt = jnp.logical_not(late)
@@ -592,12 +591,18 @@
         coef[x, 1] = -second / center
 
     spread_own(inside)
+
+    def project_last():
+        for t in range(T - LAST, T):
+            project_others(t)
+
+    pl.when(lat == 0)(project_last)
+    pl.when(wraps)(far_ready)
+    far_pass()
     inner_wait(inner2, 0, recv_sem.at[I2])
     spread_halo(inner2, 0, inner_halo)
     second_pass(inner2, i_at, inside)
     def others_image():
-        for t in range(T - LAST, T):
-            project_others(t)
         for j in range(1, X):
             x = lax.rem(chip + j, X)
             base = (j - 1) * A * E
@@ -614,8 +619,6 @@
 
             repeat(NB // 2, others_pass, 0)
 
-    pl.when(wraps)(far_ready)
-    far_pass()
     pl.when(lat == 0)(others_image)
     outer_wait(outer2, NEAR, O2)
     spread_halo(outer2, 0, outer_halo + core * NEAR, HALO - NEAR)
@@ -625,15 +628,17 @@
     s3[me] = lanes(repeat(NB, residual, zero))
     plane_send(s3.at[me], S3)
 
+    @pl.when(lat != 0)
+    def _():
+        project_last()
+        others_image()
+
     arrived(s1.at[pl.ds(0, X - 1)], recv_sem.at[S2])
     for j in range(1, X):
         chebyshev(lax.rem(chip + j, X))
     arrived(image.at[pl.ds(0, X - 1), pl.ds(0, HALO)], recv_sem.at[IM])
-    for f in range(PARTS // 2):
-        finish(f + (PARTS // 2) * core)
-    pl.when(lat != 0)(others_image)
-    for f in range(PARTS // 2):
-        finish(f + (PARTS // 2) * (1 - core))
+    for f in range(PARTS):
+        finish(f)
 
     arrived(s3.at[pl.ds(0, M - 1)], recv_sem.at[S3])
     norm = jnp.sqrt(plane_sum(s3) / (s2[chip] + 1e-06))
@@ -654,6 +659,16 @@
     for kind in (S1, S3):
         whole(s3.at[pl.ds(0, M - 1)], kind, recv_sem.at[kind]).wait_send()
     whole(s1.at[pl.ds(0, X - 1)], S2, recv_sem.at[S2]).wait_send()
+
+
+def deliver(smoothed, norm, out, res, sem):
+    copies = [
+        pltpu.make_async_copy(a, b, sem.at[i]) for i, (a, b) in enumerate([(smoothed, out), (norm, res)])
+    ]
+    for copy in copies:
+        copy.start()
+    for copy in copies:
+        copy.wait()
 
 
 def on_device(L, R, source, to_modes, from_modes, eigenvalue, shifts, weights, neighbors):
@@ -720,6 +735,19 @@
         source, weights, to_modes, from_modes, eigenvalue.reshape(1, levels),
         shifts.reshape(nodes // BLOCK, BLOCK), neighbors,
     )
+    smoothed, norm = pl.pallas_call(
+        deliver,
+        name="deliver",
+        out_shape=(
+            jax.ShapeDtypeStruct((slab, nodes), f32), jax.ShapeDtypeStruct((1, slab), f32)
+        ),
+        in_specs=[vmem, vmem],
+        out_specs=(hbm, hbm),
+        scratch_shapes=[dma((2,))],
+    )(
+        pltpu.with_memory_space_constraint(smoothed, pltpu.VMEM),
+        pltpu.with_memory_space_constraint(norm, pltpu.VMEM),
+    )
     return smoothed, norm.reshape(slab)
 
 

time: 31 us -> 30.5 us (0.984)
  local copies, waits for them, and re-layouts: 1.31 us -> 0 us
  Pallas kernels: 28.9 us -> 29.7 us
    unnamed x2 -> x0, local copies, waits for them, and re-layouts: 1.31 us -> none
    pallas_call x0 -> x1, Pallas kernels: none -> 0.81 us  [on_device(): pl.pallas_call(deliver, name='deliver', out_shape=(jax.ShapeDtypeStruct((...]
where the time goes in v6:
time: 30.5 us; the launch traced here: 30.4 us
  Pallas kernels  29.7 us (97%)
  between operations  0.64 us (2%)
    pallas_call x1, Pallas kernels, on_device(): pl.pallas_call(functools.partial(kernel, L, R, S), name='smoother', out_s...  28.9 us
    pallas_call x1, Pallas kernels, on_device(): pl.pallas_call(deliver, name='deliver', out_shape=(jax.ShapeDtypeStruct((...  0.81 us

profile of v6, /device:TPU:0, one launch (start us, length us, event | category | flops | bytes accessed | tf_op | source)
XLA Modules:
  0.0 30.4 jit_solution(4090760952531196692)
XLA Ops:
  0.6 28.9 %smoother.1 = (f32[32,4096]{1,0:T(8,128)S(1)}, f32[1,32]{1,0:T(1,128)S(1)}) custom-call(f32[32,4096]{1,0:T(8,128)} %src.1, f32[31,4096]{1,0:T(8,128)} %w_hbm.1, f32[128,128]{1,0:T(8,128)} %to_hbm.1, f32[128,128]{1,0:T(8,128)} %from_hbm.1, f32[1,128]{1,0:T(1,128)} %bitcast.4, f32[32,128]{1,0:T(8,128)} %bitcast.3, s32[31,32]{1,0:T(8,128)} %nbr_hbm.1), custom_call_target="tpu_custom_call" | custom-call | tf_op jit(solution)/shard_map/smoother/pallas_call | solution.py:693
  29.5 0.8 %deliver.1 = (f32[32,4096]{1,0:T(8,128)}, f32[1,32]{1,0:T(1,128)}) custom-call(f32[32,4096]{1,0:T(8,128)S(1)} %get-tuple-element.6.smoothed, f32[1,32]{1,0:T(1,128)S(1)} %get-tuple-element.7.norm), custom_call_target="tpu_custom_call" | custom-call | tf_op jit(solution)/shard_map/deliver/pallas_call | solution.py:738

commit v7 on v6

--- a/solution.py
+++ b/solution.py
@@ -482,7 +482,7 @@
 
         repeat(NB // 2, step, 0, UNROLL)
 
-    spread_own(outside)
+    pl.when(prompt)(functools.partial(spread_own, outside))
     inner_wait(inner1, 0, recv_sem.at[I1])
     spread_halo(inner1, 0, inner_halo)
     for t in range(T - HC, T, GROUPED):
@@ -590,6 +590,7 @@
         coef[x, 0] = (1.0 + rho_one * rho_zero) / center + second
         coef[x, 1] = -second / center
 
+    pl.when(late)(functools.partial(spread_own, outside))
     spread_own(inside)
 
     def project_last():

time: 30.5 us -> 30.5 us (level)
  no operation moved by 1% of the time
where the time goes in v7:
time: 30.5 us; the launch traced here: 30.4 us
  Pallas kernels  29.7 us (97%)
  between operations  0.64 us (2%)
    pallas_call x1, Pallas kernels, on_device(): pl.pallas_call(functools.partial(kernel, L, R, S), name='smoother', out_s...  28.9 us
    pallas_call x1, Pallas kernels, on_device(): pl.pallas_call(deliver, name='deliver', out_shape=(jax.ShapeDtypeStruct((...  0.81 us

profile of v7, /device:TPU:0, one launch (start us, length us, event | category | flops | bytes accessed | tf_op | source)
XLA Modules:
  0.0 30.4 jit_solution(5724973141701207503)
XLA Ops:
  0.6 28.9 %smoother.1 = (f32[32,4096]{1,0:T(8,128)S(1)}, f32[1,32]{1,0:T(1,128)S(1)}) custom-call(f32[32,4096]{1,0:T(8,128)} %src.1, f32[31,4096]{1,0:T(8,128)} %w_hbm.1, f32[128,128]{1,0:T(8,128)} %to_hbm.1, f32[128,128]{1,0:T(8,128)} %from_hbm.1, f32[1,128]{1,0:T(1,128)} %bitcast.4, f32[32,128]{1,0:T(8,128)} %bitcast.3, s32[31,32]{1,0:T(8,128)} %nbr_hbm.1), custom_call_target="tpu_custom_call" | custom-call | tf_op jit(solution)/shard_map/smoother/pallas_call | solution.py:694
  29.6 0.8 %deliver.1 = (f32[32,4096]{1,0:T(8,128)}, f32[1,32]{1,0:T(1,128)}) custom-call(f32[32,4096]{1,0:T(8,128)S(1)} %get-tuple-element.6.smoothed, f32[1,32]{1,0:T(1,128)S(1)} %get-tuple-element.7.norm), custom_call_target="tpu_custom_call" | custom-call | tf_op jit(solution)/shard_map/deliver/pallas_call | solution.py:739

commit v8 on v6

--- a/solution.py
+++ b/solution.py
@@ -662,9 +662,12 @@
 
 
 def deliver(smoothed, norm, out, res, sem):
-    copies = [
-        pltpu.make_async_copy(a, b, sem.at[i]) for i, (a, b) in enumerate([(smoothed, out), (norm, res)])
+    width = smoothed.shape[1] // (sem.shape[0] - 1)
+    pairs = [(norm, res)] + [
+        (smoothed.at[:, pl.ds(i * width, width)], out.at[:, pl.ds(i * width, width)])
+        for i in range(sem.shape[0] - 1)
     ]
+    copies = [pltpu.make_async_copy(a, b, sem.at[i]) for i, (a, b) in enumerate(pairs)]
     for copy in copies:
         copy.start()
     for copy in copies:
@@ -743,7 +746,7 @@
         ),
         in_specs=[vmem, vmem],
         out_specs=(hbm, hbm),
-        scratch_shapes=[dma((2,))],
+        scratch_shapes=[dma((5,))],
     )(
         pltpu.with_memory_space_constraint(smoothed, pltpu.VMEM),
         pltpu.with_memory_space_constraint(norm, pltpu.VMEM),

time: 30.5 us -> 30.5 us (level)
  no operation moved by 1% of the time
where the time goes in v8:
time: 30.5 us; the launch traced here: 30.4 us
  Pallas kernels  29.7 us (97%)
  between operations  0.64 us (2%)
    pallas_call x1, Pallas kernels, on_device(): pl.pallas_call(functools.partial(kernel, L, R, S), name='smoother', out_s...  28.9 us
    pallas_call x1, Pallas kernels, on_device(): pl.pallas_call(deliver, name='deliver', out_shape=(jax.ShapeDtypeStruct((...  0.83 us

profile of v8, /device:TPU:0, one launch (start us, length us, event | category | flops | bytes accessed | tf_op | source)
XLA Modules:
  0.0 30.4 jit_solution(7914602591233517596)
XLA Ops:
  0.6 28.9 %smoother.1 = (f32[32,4096]{1,0:T(8,128)S(1)}, f32[1,32]{1,0:T(1,128)S(1)}) custom-call(f32[32,4096]{1,0:T(8,128)} %src.1, f32[31,4096]{1,0:T(8,128)} %w_hbm.1, f32[128,128]{1,0:T(8,128)} %to_hbm.1, f32[128,128]{1,0:T(8,128)} %from_hbm.1, f32[1,128]{1,0:T(1,128)} %bitcast.4, f32[32,128]{1,0:T(8,128)} %bitcast.3, s32[31,32]{1,0:T(8,128)} %nbr_hbm.1), custom_call_target="tpu_custom_call" | custom-call | tf_op jit(solution)/shard_map/smoother/pallas_call | solution.py:696
  29.5 0.8 %deliver.1 = (f32[32,4096]{1,0:T(8,128)}, f32[1,32]{1,0:T(1,128)}) custom-call(f32[32,4096]{1,0:T(8,128)S(1)} %get-tuple-element.6.smoothed, f32[1,32]{1,0:T(1,128)S(1)} %get-tuple-element.7.norm), custom_call_target="tpu_custom_call" | custom-call | tf_op jit(solution)/shard_map/deliver/pallas_call | solution.py:741
